TPU v7x, 512 devices: a whole 4x8x8 slice. The times are simulated.
512 devices in a mesh: tm: 32 (over z, y_lo), row: 16 (over x, y_hi, core).
Axes of the slice: x: 4, y: 8 (y_hi: 2, y_lo: 4; y = y_hi * 4 + y_lo), z: 8, core: 2. Of those that a mesh axis runs over, the one named last changes fastest.
Arguments:
- output_first_half: bfloat16 [64, 16, 64, 320], P('tm', 'row'), may hold values from -6 to 6
- y_second: bfloat16 [64, 16, 64, 320], P('tm', 'row'), may hold values from -6 to 6
- cot_first: bfloat16 [64, 16, 64, 320], P('tm', 'row'), may hold values from -6 to 6
- cot_second: bfloat16 [64, 16, 64, 320], P('tm', 'row'), may hold values from -6 to 6
- weight_space: bfloat16 [3, 3, 2, 160, 160], replicated, may hold values from -0.15625 to 0.15625
- temporal_weight: bfloat16 [3, 5, 128, 128], replicated, may hold values from -0.3125 to 0.3125
Outputs:
- x_first: bfloat16 [64, 16, 64, 320], P('tm', 'row')
- x_second: bfloat16 [64, 16, 64, 320], P('tm', 'row')
- grad_first: bfloat16 [64, 16, 64, 320], P('tm', 'row')
- grad_second: bfloat16 [64, 16, 64, 320], P('tm', 'row')
- spatial_weight_gradient: float32 [460800], P(('tm', 'row'))
- grad_time: float32 [245760], P(('tm', 'row'))
All inputs are finite; a program needn't handle non-finite values.
Results may differ from a plain program's by a relative error of at most 0.007.
Values may be sent and summed in bfloat16 or wider, within the bound.
A program may use at most 64 MiB of HBM per device.

v0:
```python
import math

import jax
import jax.numpy as jnp
from jax import lax
from jax.sharding import PartitionSpec as P

HAAR = 0.7071067811865476


def extended(x, sides, width):
    for axis, dim in sides:
        peers, length = (lax.axis_size(axis), x.shape[dim])
        up = [(i, (i + 1) % peers) for i in range(peers - 1)]
        down = [(j, i) for i, j in up]
        last = lax.slice_in_dim(x, length - width, length, axis=dim)
        initial = lax.slice_in_dim(x, 0, width, axis=dim)
        before = lax.ppermute(last, axis, up)
        after = lax.ppermute(initial, axis, down)
        x = jnp.concatenate([before, x, after], axis=dim)
    return x


def haar_pair_squeeze(input_frames):
    even_frames = input_frames[0::2].astype(jnp.float32)
    odd_frames = input_frames[1::2].astype(jnp.float32)
    return jnp.concatenate(
        [(even_frames + odd_frames) * HAAR, (even_frames - odd_frames) * HAAR], axis=-1
    )


def unsqueeze_pairs(packed):
    half_ch = packed.shape[-1] // 2
    low_band = packed[..., :half_ch]
    high_band = packed[..., half_ch:]
    stacked = jnp.stack([(low_band + high_band) * HAAR, (low_band - high_band) * HAAR], axis=1)
    return stacked.reshape((2 * low_band.shape[0],) + low_band.shape[1:])


def silu_slope(values):
    sigmoid_v = jax.nn.sigmoid(values)
    return sigmoid_v * (1.0 + values * (1.0 - sigmoid_v))


def split_groups(tensor, groups):
    return tensor.reshape(tensor.shape[:-1] + (groups, tensor.shape[-1] // groups))


def merge_groups(tensor):
    return tensor.reshape(tensor.shape[:-2] + (tensor.shape[-2] * tensor.shape[-1],))


def time_apply(act_ext, temporal_weight):
    length = act_ext.shape[0] - 2
    groups = temporal_weight.shape[1]
    summed = None
    for offset in range(3):
        window = split_groups(act_ext[offset : offset + length], groups)
        partial_sum = jnp.einsum(
            "t...gi,gio->t...go",
            window,
            temporal_weight[offset],
            preferred_element_type=jnp.float32,
        )
        summed = partial_sum if summed is None else summed + partial_sum
    return merge_groups(summed)


def time_back(cot_ext, temporal_weight):
    length = cot_ext.shape[0] - 2
    groups = temporal_weight.shape[1]
    summed = None
    for offset in range(3):
        window = split_groups(cot_ext[2 - offset : 2 - offset + length], groups)
        partial_sum = jnp.einsum(
            "t...go,gio->t...gi",
            window,
            temporal_weight[offset],
            preferred_element_type=jnp.float32,
        )
        summed = partial_sum if summed is None else summed + partial_sum
    return merge_groups(summed)


def time_wgrad(act_ext, cot_inner, groups):
    length = cot_inner.shape[0]
    cot_split = split_groups(cot_inner, groups)
    result = []
    for offset in range(3):
        window = split_groups(act_ext[offset : offset + length], groups)
        result.append(
            jnp.einsum("t...gi,t...go->gio", window, cot_split, preferred_element_type=jnp.float32)
        )
    return jnp.stack(result)


def time_core(y_ext, cot_ext, temporal_weight):
    squeezed = haar_pair_squeeze(y_ext)
    act_time = jax.nn.silu(squeezed).astype(jnp.bfloat16)
    temporal_cotangent = haar_pair_squeeze(cot_ext).astype(jnp.bfloat16)
    branch_time = unsqueeze_pairs(time_apply(act_time, temporal_weight)).astype(jnp.bfloat16)
    back_sum = time_back(temporal_cotangent, temporal_weight) * silu_slope(squeezed[1:-1])
    back_time = unsqueeze_pairs(back_sum).astype(jnp.bfloat16)
    sum_time = time_wgrad(act_time, temporal_cotangent[1:-1], temporal_weight.shape[1])
    return (branch_time, back_time, sum_time)


def space_apply(act_pad, weight_space):
    rows_in = act_pad.shape[-3] - 2
    cols_in = act_pad.shape[-2] - 2
    groups = weight_space.shape[2]
    summed = None
    for row_tap in range(3):
        for col_tap in range(3):
            window = split_groups(
                act_pad[..., row_tap : row_tap + rows_in, col_tap : col_tap + cols_in, :], groups
            )
            partial_sum = jnp.einsum(
                "...gi,gio->...go",
                window,
                weight_space[row_tap, col_tap],
                preferred_element_type=jnp.float32,
            )
            summed = partial_sum if summed is None else summed + partial_sum
    return merge_groups(summed)


def space_back(cot_pad, weight_space):
    rows_in = cot_pad.shape[-3] - 2
    cols_in = cot_pad.shape[-2] - 2
    groups = weight_space.shape[2]
    summed = None
    for row_tap in range(3):
        for col_tap in range(3):
            window = cot_pad[
                ..., 2 - row_tap : 2 - row_tap + rows_in, 2 - col_tap : 2 - col_tap + cols_in, :
            ]
            window = split_groups(window, groups)
            partial_sum = jnp.einsum(
                "...go,gio->...gi",
                window,
                weight_space[row_tap, col_tap],
                preferred_element_type=jnp.float32,
            )
            summed = partial_sum if summed is None else summed + partial_sum
    return merge_groups(summed)


def space_wgrad(act_pad, cot_inner, groups):
    rows_in = cot_inner.shape[-3]
    cols_in = cot_inner.shape[-2]
    cot_split = split_groups(cot_inner, groups)
    result = []
    for row_tap in range(3):
        row_list = []
        for col_tap in range(3):
            window = split_groups(
                act_pad[..., row_tap : row_tap + rows_in, col_tap : col_tap + cols_in, :], groups
            )
            row_list.append(
                jnp.einsum(
                    "...gi,...go->gio", window, cot_split, preferred_element_type=jnp.float32
                )
            )
        result.append(jnp.stack(row_list))
    return jnp.stack(result)


def per_device(output_first_half, y_second, cot_first, cot_second, weight_space, temporal_weight):
    joined = jnp.stack([output_first_half, cot_second])
    rimmed = extended(joined, (("tm", 1),), 2)
    branch_time, back_time, sum_time = time_core(rimmed[0], rimmed[1], temporal_weight)
    cells_all = (
        output_first_half.shape[0]
        * output_first_half.shape[1]
        * output_first_half.shape[2]
        * lax.axis_size("tm")
        * lax.axis_size("row")
    )
    factor = 1.0 / math.sqrt(cells_all)
    recovered = (y_second.astype(jnp.float32) - branch_time.astype(jnp.float32)).astype(
        jnp.bfloat16
    )
    first_grad = (cot_first.astype(jnp.float32) + back_time.astype(jnp.float32)).astype(
        jnp.bfloat16
    )
    stacked = jnp.stack([recovered, first_grad])
    row_ext = extended(stacked, (("row", 2),), 1)
    col_pad = ((0, 0), (0, 0), (1, 1), (0, 0))
    act_pad = jax.nn.silu(jnp.pad(row_ext[0], col_pad).astype(jnp.float32)).astype(jnp.bfloat16)
    cot_pad = jnp.pad(row_ext[1], col_pad)
    first_rec = (output_first_half.astype(jnp.float32) - space_apply(act_pad, weight_space)).astype(
        jnp.bfloat16
    )
    back_sum = space_back(cot_pad, weight_space) * silu_slope(recovered.astype(jnp.float32))
    second_grad = (cot_second.astype(jnp.float32) + back_sum).astype(jnp.bfloat16)
    sum_space = space_wgrad(act_pad, first_grad, weight_space.shape[2])
    space_share, time_share = (
        lax.psum_scatter(sum_space.reshape(-1), ("tm", "row"), scatter_dimension=0, tiled=True),
        lax.psum_scatter(sum_time.reshape(-1), ("tm", "row"), scatter_dimension=0, tiled=True),
    )
    return (
        first_rec,
        recovered,
        first_grad,
        second_grad,
        space_share * factor,
        time_share * factor,
    )


def solution(mesh):
    in_specs = (
        P("tm", "row", None, None),
        P("tm", "row", None, None),
        P("tm", "row", None, None),
        P("tm", "row", None, None),
        P(),
        P(),
    )
    out_specs = (
        P("tm", "row", None, None),
        P("tm", "row", None, None),
        P("tm", "row", None, None),
        P("tm", "row", None, None),
        P(("tm", "row")),
        P(("tm", "row")),
    )
    return jax.shard_map(
        per_device, mesh=mesh, in_specs=in_specs, out_specs=out_specs, check_vma=False
    )
```

profile of v0, /device:TPU:1, one launch (start us, length us, event | category | flops | bytes accessed | tf_op | source)
XLA Modules:
  0.0 373.8 jit_solution(3735098838429851803)
XLA Ops:
  8.2 1.3 collective-permute-start.1
  9.5 4.7 %collective-permute-start = (bf16[2,2,1,64,320]{4,3,1,2,0:T(8,128)(2,1)S(1)}, bf16[2,2,1,64,320]{4,3,1,2,0:T(8,128)(2,1)S(1)}, u32[]{:S(2)}, u32[]{:S(2)}) collective-permute-start(bf16[2,2,1,64,320]{4,3,1,2,0:T(8,128)(2,1)S(1)} %pad_maximum_fusion.5), channel_id=1, source_target_pairs={{0,16},{16,32},{32,48},{48,64},{64,80},{80,96},{96,112},{112,128},... | collective-permute-start | bytes 491528 | tf_op jit(solution)/shard_map/ppermute | solution.py:18
  14.2 1.1 collective-permute-done.1
  15.3 1.5 collective-permute-done
  21.3 12.0 %collective-permute-start.3 = (bf16[2,2,1,64,320]{4,3,1,2,0:T(8,128)(2,1)S(1)}, bf16[2,2,1,64,320]{4,3,1,2,0:T(8,128)(2,1)S(1)}, u32[]{:S(2)}, u32[]{:S(2)}) collective-permute-start(bf16[2,2,1,64,320]{4,3,1,2,0:T(8,128)(2,1)S(1)} %pad_maximum_fusion.6), channel_id=1, source_target_pairs={{1,0},{2,1},{3,2},{4,3},{5,4},{6,5},{7,6},{8,7},{9,8},{10,9},{11,1... | collective-permute-start | bytes 491528 | tf_op jit(solution)/shard_map/ppermute | solution.py:19
  33.3 1.9 collective-permute-start.2
  41.2 1.1 convolution_add_fusion.15
  42.6 1.1 convolution_add_fusion.14
  44.1 1.1 convolution_add_fusion.13
  45.5 1.1 convolution_add_fusion.12
  47.0 1.1 convolution_add_fusion.11
  48.4 1.8 convolution_add_fusion.10
  50.6 1.2 convolution_add_fusion.9
  54.8 1.8 fusion.43
  56.6 1.6 reshape.407
  58.2 1.7 reshape.408
  59.9 1.6 reshape.409
  63.1 3.4 reshape.417
  66.5 1.4 convolution_add_fusion.7
  67.9 1.2 convolution_add_fusion.6
  69.1 1.1 convolution_add_fusion.5
  74.6 289.7 %all-reduce.7.cloned.1.call-done = (f32[460800]{0:T(1024)}, f32[245760]{0:T(1024)}) async-done(((f32[460800]{0:T(1024)}, f32[245760]{0:T(1024)}), (f32[460800]{0:T(1024)}, f32[245760]{0:T(1024)})) %all-reduce.7.cloned.1.call-update) | async-done | bytes 2826256
  364.3 1.4 dynamic-slice_multiply_fusion
  365.6 1.3 dynamic-slice_multiply_fusion.1
  (110 shorter events, 22.0 us)
Async XLA Ops:
  7.2 357.1 %all-reduce.7.cloned.1.call-start = ((), (), s32[]{:S(2)}) async-start(), calls=%async_computation | async-start | bytes 5652480
  8.2 7.1 %collective-permute-start.1 = (bf16[2,2,1,64,320]{4,3,1,2,0:T(8,128)(2,1)S(1)}, bf16[2,2,1,64,320]{4,3,1,2,0:T(8,128)(2,1)S(1)}, u32[]{:S(2)}, u32[]{:S(2)}) collective-permute-start(bf16[2,2,1,64,320]{4,3,1,2,0:T(8,128)(2,1)S(1)} %pad_maximum_fusion.5), channel_id=1, source_target_pairs={{16,0},{32,16},{48,32},{64,48},{80,64},{96,80},{112,96},{128,112},... | collective-permute-start | bytes 491528 | tf_op jit(solution)/shard_map/ppermute | solution.py:19
  9.5 7.3 %collective-permute-start = (bf16[2,2,1,64,320]{4,3,1,2,0:T(8,128)(2,1)S(1)}, bf16[2,2,1,64,320]{4,3,1,2,0:T(8,128)(2,1)S(1)}, u32[]{:S(2)}, u32[]{:S(2)}) collective-permute-start(bf16[2,2,1,64,320]{4,3,1,2,0:T(8,128)(2,1)S(1)} %pad_maximum_fusion.5), channel_id=1, source_target_pairs={{0,16},{16,32},{32,48},{48,64},{64,80},{80,96},{96,112},{112,128},... | collective-permute-start | bytes 491528 | tf_op jit(solution)/shard_map/ppermute | solution.py:18
  17.9 1.0 copy-start.1
  20.1 1.1 copy-start.3
  20.2 1.0 copy-start.11
  21.3 16.5 %collective-permute-start.3 = (bf16[2,2,1,64,320]{4,3,1,2,0:T(8,128)(2,1)S(1)}, bf16[2,2,1,64,320]{4,3,1,2,0:T(8,128)(2,1)S(1)}, u32[]{:S(2)}, u32[]{:S(2)}) collective-permute-start(bf16[2,2,1,64,320]{4,3,1,2,0:T(8,128)(2,1)S(1)} %pad_maximum_fusion.6), channel_id=1, source_target_pairs={{1,0},{2,1},{3,2},{4,3},{5,4},{6,5},{7,6},{8,7},{9,8},{10,9},{11,1... | collective-permute-start | bytes 491528 | tf_op jit(solution)/shard_map/ppermute | solution.py:19
  33.3 4.9 %collective-permute-start.2 = (bf16[2,2,1,64,320]{4,3,1,2,0:T(8,128)(2,1)S(1)}, bf16[2,2,1,64,320]{4,3,1,2,0:T(8,128)(2,1)S(1)}, u32[]{:S(2)}, u32[]{:S(2)}) collective-permute-start(bf16[2,2,1,64,320]{4,3,1,2,0:T(8,128)(2,1)S(1)} %pad_maximum_fusion.6), channel_id=1, source_target_pairs={{0,1},{1,2},{2,3},{3,4},{4,5},{5,6},{6,7},{7,8},{8,9},{9,10},{10,1... | collective-permute-start | bytes 491528 | tf_op jit(solution)/shard_map/ppermute | solution.py:18
  53.7 7.8 %copy-start.10 = (bf16[2,1,64,320]{3,2,0,1:T(8,128)(2,1)S(1)}, bf16[2,1,64,320]{3,2,0,1:T(8,128)(2,1)}, u32[]{:S(2)}) copy-start(bf16[2,1,64,320]{3,2,0,1:T(8,128)(2,1)} %get-tuple-element.45) | copy-start | bytes 245764
  66.5 2.6 copy-start
  66.5 3.7 copy-start.5
  70.5 0.9 copy-start.9
  70.5 1.0 copy-start.8
  70.5 1.1 copy-start.7
  70.5 1.2 copy-start.6
  72.2 0.9 copy-start.2
  72.3 1.5 copy-start.4
  72.3 1.5 copy-start.12
Sparse Core Ops, SparseCore 0:
  70.6 293.6 all-reduce.6
where the time goes:
time: 375 us; the launch traced here: 374 us
  waiting for transfers between devices  293 us (78%)
  matrix products  20.4 us (5%)
  starting transfers between devices  19.9 us (5%)
  local copies, waits for them, and re-layouts  16.5 us (4%)
  between operations  14.7 us (4%)
  other arithmetic  9.74 us (3%)
    unnamed x2, waiting for transfers between devices  290 us
    ppermute x2, starting transfers between devices, extended(): after = lax.ppermute(initial, axis, down)  13.3 us
    dot_general x9, matrix products, space_apply(): jnp.einsum('...gi,gio->...go', window, weight_space[row_tap, col_tap], pr...  9.76 us
    another operation x24, local copies, waits for them, and re-layouts  9.59 us
  transfers between devices with their start and end apart: 5, of which 4 were waited for; matrix products, arithmetic and copies ran while one was open for 2% of the time, Pallas kernels for 0%

commit v1 on v0

--- a/solution.py
+++ b/solution.py
@@ -3,9 +3,181 @@
 import jax
 import jax.numpy as jnp
 from jax import lax
+from jax.experimental import pallas as pl
+from jax.experimental.pallas import tpu as pltpu
 from jax.sharding import PartitionSpec as P
 
 HAAR = 0.7071067811865476
+MESH = pl.DeviceIdType.MESH
+F32, BF16 = jnp.float32, jnp.bfloat16
+
+
+def place():
+    tm, row = lax.axis_index("tm"), lax.axis_index("row")
+    return tm // 4, tm % 4, row // 4, (row // 2) % 2, row % 2
+
+
+def ident(z, yl, x, yh, c):
+    return (z * 4 + yl, x * 4 + yh * 2 + c)
+
+
+def greet(z, yl, x, yh, c):
+    peers = []
+    for dx in range(4):
+        for h in range(2):
+            for dc in range(2):
+                if dx or h or dc:
+                    peers.append(ident(z, yl, (x + dx) % 4, (yh + h) % 2, (c + dc) % 2))
+    for j in range(1, 4):
+        for h in range(2):
+            peers.append(ident(z, (yl + j) % 4, x, (yh + h) % 2, c))
+    for d in range(1, 8):
+        peers.append(ident((z + d) % 8, yl, x, yh, c))
+    barrier = pltpu.get_barrier_semaphore()
+    for peer in peers:
+        pl.semaphore_signal(barrier, inc=1, device_id=peer, device_id_type=MESH)
+    pl.semaphore_wait(barrier, len(peers))
+
+
+def sum_kernel(p, out, r0, s0, r1, s1, r2, s2, r3, fin, q_snd, q_rcv, x_snd, x_rcv, y_snd, y_rcv, z_snd, z_rcv, g_snd, g_rcv):
+    z, yl, x, yh, c = place()
+    greet(z, yl, x, yh, c)
+
+    def send(src, dst, snd, rcv, peer):
+        return pltpu.make_async_remote_copy(src_ref=src, dst_ref=dst, send_sem=snd, recv_sem=rcv, device_id=peer, device_id_type=MESH)
+
+    started = []
+    first = []
+    for k in (1, 2, 3, 0):
+        xp = (x + k) % 4
+        copy = send(p.at[1 - c, xp], r0.at[xp], q_snd.at[k], q_rcv.at[k], ident(z, yl, x, yh, 1 - c))
+        copy.start()
+        first.append(copy)
+    second = {}
+    for n, k in enumerate((1, 2, 3, 0)):
+        xp = (x + k) % 4
+        first[n].wait_recv()
+        for j in (1, 2, 3, 0):
+            yp = (yl + j) % 4
+            s0[xp, yp] = (p[c, xp, yp].astype(F32) + r0[xp, yp].astype(F32)).astype(BF16)
+            if k:
+                copy = send(s0.at[xp, yp], r1.at[k - 1, yp], x_snd.at[k - 1, j], x_rcv.at[k - 1, j], ident(z, yl, xp, yh, c))
+                copy.start()
+                second[k, j] = copy
+    third = {}
+    for j in (1, 2, 3, 0):
+        yp = (yl + j) % 4
+        for k in (1, 2, 3):
+            second[k, j].wait_recv()
+        total = s0[x, yp].astype(F32)
+        for k in (1, 2, 3):
+            total += r1[k - 1, yp].astype(F32)
+        s1[yp] = total.astype(BF16)
+        for h in (1, 0):
+            if j or h:
+                hp = (yh + h) % 2
+                copy = send(s1.at[yp, pl.ds(hp * 4, 4)], r2.at[2 * j + h], y_snd.at[2 * j + h], y_rcv.at[2 * j + h], ident(z, yp, x, hp, c))
+                copy.start()
+                third[j, h] = copy
+    total = s1[yl, pl.ds(yh * 4, 4)].astype(F32)
+    for j, h in third:
+        third[j, h].wait_recv()
+    for j, h in third:
+        total += r2[2 * j + h].astype(F32)
+    s2[...] = total.astype(BF16)
+    mine = z // 4 == yh
+    for d in range(1, 8):
+        zp = (z + d) % 8
+
+        @pl.when(zp // 4 == yh)
+        def _():
+            send(s2.at[zp % 4], r3.at[d - 1], z_snd.at[d - 1], z_rcv.at[d - 1], ident(zp, yl, x, yh, c)).start()
+
+    @pl.when(mine)
+    def _():
+        for d in range(1, 8):
+            send(s2.at[0], r3.at[d - 1], z_snd.at[d - 1], z_rcv.at[d - 1], ident((z + d) % 8, yl, x, yh, c)).wait_recv()
+        last = s2[z % 4].astype(F32)
+        for d in range(1, 8):
+            last += r3[d - 1].astype(F32)
+        fin[c * 4 + x] = last
+        for dx in range(4):
+            for h in range(2):
+                for dc in range(2):
+                    if dx or h or dc:
+                        n = dx * 2 + dc
+                        send(fin.at[c * 4 + x], fin.at[c * 4 + x], g_snd.at[n, h], g_rcv.at[n], ident(z, yl, (x + dx) % 4, (yh + h) % 2, (c + dc) % 2)).start()
+
+    for dx in range(4):
+        for dc in range(2):
+            n = dx * 2 + dc
+            src = ((c + dc) % 2) * 4 + (x - dx) % 4
+
+            def wait():
+                send(fin.at[src], fin.at[src], g_snd.at[n, 0], g_rcv.at[n], ident(z, yl, (x + dx) % 4, yh, (c + dc) % 2)).wait_recv()
+
+            if n:
+                wait()
+            else:
+                pl.when(jnp.logical_not(mine))(lambda: send(fin.at[src], fin.at[src], g_snd.at[0, 1], g_rcv.at[0], ident(z, yl, x, 1 - yh, c)).wait_recv())
+    out[...] = fin[...]
+    for copy in first + list(second.values()) + list(third.values()):
+        copy.wait_send()
+    for d in range(1, 8):
+        zp = (z + d) % 8
+
+        @pl.when(zp // 4 == yh)
+        def _():
+            send(s2.at[zp % 4], r3.at[d - 1], z_snd.at[d - 1], z_rcv.at[d - 1], ident(zp, yl, x, yh, c)).wait_send()
+
+    @pl.when(mine)
+    def _():
+        for dx in range(4):
+            for h in range(2):
+                for dc in range(2):
+                    if dx or h or dc:
+                        n = dx * 2 + dc
+                        send(fin.at[c * 4 + x], fin.at[c * 4 + x], g_snd.at[n, h], g_rcv.at[n], ident(z, yl, (x + dx) % 4, (yh + h) % 2, (c + dc) % 2)).wait_send()
+
+
+def summed(p):
+    dma = pltpu.SemaphoreType.DMA
+    out = pl.pallas_call(
+        sum_kernel,
+        out_shape=jax.ShapeDtypeStruct((8, 3, 8, 128), F32),
+        in_specs=[pl.BlockSpec(memory_space=pltpu.VMEM)],
+        out_specs=pl.BlockSpec(memory_space=pltpu.VMEM),
+        scratch_shapes=[
+            pltpu.VMEM((4, 4, 8, 3, 8, 128), BF16),
+            pltpu.VMEM((4, 4, 8, 3, 8, 128), BF16),
+            pltpu.VMEM((3, 4, 8, 3, 8, 128), BF16),
+            pltpu.VMEM((4, 8, 3, 8, 128), BF16),
+            pltpu.VMEM((8, 4, 3, 8, 128), BF16),
+            pltpu.VMEM((4, 3, 8, 128), BF16),
+            pltpu.VMEM((7, 3, 8, 128), BF16),
+            pltpu.VMEM((8, 3, 8, 128), F32),
+            dma((4,)), dma((4,)), dma((3, 4)), dma((3, 4)), dma((8,)), dma((8,)), dma((7,)), dma((7,)), dma((8, 2)), dma((8,)),
+        ],
+        compiler_params=pltpu.CompilerParams(collective_id=3, has_side_effects=True),
+        name="sum_terms",
+    )(p)
+    return out.reshape(192, 128)
+
+
+def packed(sum_space, sum_time):
+    s = sum_space.reshape(32, 90, 160)
+    s = jnp.pad(s, ((0, 0), (0, 6), (0, 0)))
+    rest = s[:, :, 128:].reshape(32, 4, 24, 32).transpose(0, 2, 1, 3).reshape(32, 24, 128)
+    t = jnp.pad(sum_time.reshape(32, 60, 128), ((0, 0), (0, 12), (0, 0)))
+    p = jnp.concatenate([s[:, :, :128], rest, t], axis=1).astype(BF16)
+    return p.reshape(8, 4, 2, 4, 3, 8, 128).transpose(2, 3, 1, 0, 4, 5, 6)
+
+
+def shares(chunk, row):
+    rest = chunk[96:120].reshape(24, 4, 32).transpose(1, 0, 2).reshape(96, 32)
+    space = jnp.concatenate([chunk[:90], rest[:90]], axis=1).reshape(-1)
+    time = chunk[120:180].reshape(-1)
+    return lax.dynamic_slice(space, (900 * row,), (900,)), lax.dynamic_slice(time, (480 * row,), (480,))
 
 
 def extended(x, sides, width):
@@ -195,10 +367,8 @@
     back_sum = space_back(cot_pad, weight_space) * silu_slope(recovered.astype(jnp.float32))
     second_grad = (cot_second.astype(jnp.float32) + back_sum).astype(jnp.bfloat16)
     sum_space = space_wgrad(act_pad, first_grad, weight_space.shape[2])
-    space_share, time_share = (
-        lax.psum_scatter(sum_space.reshape(-1), ("tm", "row"), scatter_dimension=0, tiled=True),
-        lax.psum_scatter(sum_time.reshape(-1), ("tm", "row"), scatter_dimension=0, tiled=True),
-    )
+    chunk = summed(packed(sum_space, sum_time))
+    space_share, time_share = shares(chunk, lax.axis_index("row"))
     return (
         first_rec,
         recovered,

time: 375 us -> 118 us (0.31)
  waiting for transfers between devices: 293 us -> 2.59 us
  Pallas kernels: 0 us -> 50.3 us
  between operations: 14.7 us -> 1.6 us
  matrix products: 20.4 us -> 7.45 us
  local copies, waits for them, and re-layouts: 16.5 us -> 24 us
    unnamed x2 -> x0, waiting for transfers between devices: 290 us -> none
    pallas_call x0 -> x1, Pallas kernels: none -> 50.3 us  [summed(): pl.pallas_call(sum_kernel, out_shape=jax.ShapeDtypeStruct((8, 3, 8, 128),...]
    dot_general x9, matrix products: 9.76 us -> 1.57 us  [space_apply(): jnp.einsum('...gi,gio->...go', window, weight_space[row_tap, col_tap], pr...]
    another operation x24 -> x25, local copies, waits for them, and re-layouts: 9.59 us -> 2.74 us
    reshape x2 -> x11, local copies, waits for them, and re-layouts: 3.48 us -> 8.84 us  [the longest x2 3.94 us: packed(): s = sum_space.reshape(32, 90, 160)]
    dot_general x9, matrix products: 6.51 us -> 1.79 us  [space_back(): jnp.einsum('...go,gio->...gi', window, weight_space[row_tap, col_tap], pr...]
  transfers between devices with their start and end apart: 5 -> 4, of which waited for: 4 -> 2; matrix products, arithmetic and copies ran while one was open for 2% -> 4% of each run, Pallas kernels for 0% -> 0%
where the time goes in v1:
time: 118 us; the launch traced here: 117 us
  Pallas kernels  50.3 us (43%)
  local copies, waits for them, and re-layouts  24 us (20%)
  starting transfers between devices  20 us (17%)
  other arithmetic  10.9 us (9%)
  matrix products  7.45 us (6%)
  waiting for transfers between devices  2.59 us (2%)
  between operations  1.6 us (1%)
    pallas_call x1, Pallas kernels, summed(): pl.pallas_call(sum_kernel, out_shape=jax.ShapeDtypeStruct((8, 3, 8, 128),...  50.3 us
    ppermute x2, starting transfers between devices, extended(): after = lax.ppermute(initial, axis, down)  13.3 us
    ppermute x2, starting transfers between devices, extended(): before = lax.ppermute(last, axis, up)  6.76 us
    reshape x2, local copies, waits for them, and re-layouts, packed(): s = sum_space.reshape(32, 90, 160)  3.94 us
    convert_element_type x1, local copies, waits for them, and re-layouts, packed(): p = jnp.concatenate([s[:, :, :128], rest, t], axis=1).astype(BF16)  3 us
    concatenate x1, local copies, waits for them, and re-layouts, packed(): p = jnp.concatenate([s[:, :, :128], rest, t], axis=1).astype(BF16)  2.91 us
    another operation x25, local copies, waits for them, and re-layouts  2.74 us
    reshape x2, local copies, waits for them, and re-layouts, packed(): t = jnp.pad(sum_time.reshape(32, 60, 128), ((0, 0), (0, 12), (0, 0)))  2.63 us
  transfers between devices with their start and end apart: 4, of which 2 were waited for; matrix products, arithmetic and copies ran while one was open for 4% of the time, Pallas kernels for 0%

profile of v1, /device:TPU:1, one launch (start us, length us, event | category | flops | bytes accessed | tf_op | source)
XLA Modules:
  0.0 116.9 jit_solution(4642442883821315727)
XLA Ops:
  0.6 1.0 pad_maximum_fusion.5
  1.6 1.3 %collective-permute-start.1 = (bf16[2,2,1,64,320]{4,3,1,2,0:T(8,128)(2,1)S(1)}, bf16[2,2,1,64,320]{4,3,1,2,0:T(8,128)(2,1)S(1)}, u32[]{:S(2)}, u32[]{:S(2)}) collective-permute-start(bf16[2,2,1,64,320]{4,3,1,2,0:T(8,128)(2,1)S(1)} %pad_maximum_fusion.5), channel_id=1, source_target_pairs={{16,0},{32,16},{48,32},{64,48},{80,64},{96,80},{112,96},{128,112},... | collective-permute-start | bytes 491528 | tf_op jit(solution)/shard_map/ppermute | solution.py:191
  2.9 4.7 %collective-permute-start = (bf16[2,2,1,64,320]{4,3,1,2,0:T(8,128)(2,1)S(1)}, bf16[2,2,1,64,320]{4,3,1,2,0:T(8,128)(2,1)S(1)}, u32[]{:S(2)}, u32[]{:S(2)}) collective-permute-start(bf16[2,2,1,64,320]{4,3,1,2,0:T(8,128)(2,1)S(1)} %pad_maximum_fusion.5), channel_id=1, source_target_pairs={{0,16},{16,32},{32,48},{48,64},{64,80},{80,96},{96,112},{112,128},... | collective-permute-start | bytes 491528 | tf_op jit(solution)/shard_map/ppermute | solution.py:190
  7.6 1.1 collective-permute-done.1
  8.7 1.5 %collective-permute-done = bf16[2,2,1,64,320]{4,3,1,2,0:T(8,128)(2,1)S(1)} collective-permute-done((bf16[2,2,1,64,320]{4,3,1,2,0:T(8,128)(2,1)S(1)}, bf16[2,2,1,64,320]{4,3,1,2,0:T(8,128)(2,1)S(1)}, u32[]{:S(2)}, u32[]{:S(2)}) %collective-permute-start) | collective-permute-done | bytes 163872 | tf_op jit(solution)/shard_map/ppermute | solution.py:190
  10.2 1.1 pad_maximum_fusion.1
  14.7 12.0 %collective-permute-start.3 = (bf16[2,2,1,64,320]{4,3,1,2,0:T(8,128)(2,1)S(1)}, bf16[2,2,1,64,320]{4,3,1,2,0:T(8,128)(2,1)S(1)}, u32[]{:S(2)}, u32[]{:S(2)}) collective-permute-start(bf16[2,2,1,64,320]{4,3,1,2,0:T(8,128)(2,1)S(1)} %pad_maximum_fusion.6), channel_id=1, source_target_pairs={{1,0},{2,1},{3,2},{4,3},{5,4},{6,5},{7,6},{8,7},{9,8},{10,9},{11,1... | collective-permute-start | bytes 491528 | tf_op jit(solution)/shard_map/ppermute | solution.py:191
  26.7 2.1 %collective-permute-start.2 = (bf16[2,2,1,64,320]{4,3,1,2,0:T(8,128)(2,1)S(1)}, bf16[2,2,1,64,320]{4,3,1,2,0:T(8,128)(2,1)S(1)}, u32[]{:S(2)}, u32[]{:S(2)}) collective-permute-start(bf16[2,2,1,64,320]{4,3,1,2,0:T(8,128)(2,1)S(1)} %pad_maximum_fusion.6), channel_id=1, source_target_pairs={{0,1},{1,2},{2,3},{3,4},{4,5},{5,6},{6,7},{7,8},{8,9},{9,10},{10,1... | collective-permute-start | bytes 491528 | tf_op jit(solution)/shard_map/ppermute | solution.py:190
  29.8 2.5 %copy.163 = bf16[32,60,128]{1,0,2:T(8,128)(2,1)} copy(bf16[32,60,128]{2,1,0:T(8,128)(2,1)S(1)} %reshape.449) | data formatting | bytes 983040 | tf_op jit(solution)/shard_map/reshape | solution.py:171
  37.4 1.5 %pad_maximum_fusion = bf16[3,3,2,160,160]{4,3,2,1,0:T(8,128)(2,1)} fusion(bf16[1,3,2,160,160]{4,3,2,1,0:T(8,128)(2,1)S(1)} %maximum_bitcast_fusion.2, bf16[1,3,2,160,160]{4,3,2,1,0:T(8,128)(2,1)S(1)} %maximum_bitcast_fusion.1, bf16[1,3,2,160,160]{4,3,2,1,0:T(8,128)(2,1)S(1)} %maximum_bitcast_fusion), kind=kLoop, calls=%fused_computation.2 | loop fusion | flops 921600 | bytes 1843200 | tf_op jit(solution)/shard_map/stack | solution.py:338
  38.9 2.5 %reshape.485 = bf16[32,90,160]{2,1,0:T(8,128)(2,1)S(1)} reshape(bf16[3,3,2,160,160]{4,3,2,1,0:T(8,128)(2,1)} %pad_maximum_fusion) | data formatting | bytes 1843200 | tf_op jit(solution)/shard_map/reshape | solution.py:168
  41.4 1.4 %copy.190 = bf16[32,90,160]{1,0,2:T(8,128)(2,1)S(1)} copy(bf16[32,90,160]{2,1,0:T(8,128)(2,1)S(1)} %reshape.485) | data formatting | bytes 1843200 | tf_op jit(solution)/shard_map/reshape | solution.py:168
  43.7 0.7 copy.156
  44.5 1.1 copy-done.1
  45.6 1.5 %fusion.1 = bf16[32,192,128]{1,0,2:T(8,128)(2,1)S(1)} fusion(bf16[32,60,128]{1,0,2:T(8,128)(2,1)S(1)} %copy-done.1, bf16[32,24,128]{1,0,2:T(8,128)(2,1)S(1)} %bitcast.370, bf16[32,96,128]{1,0,2:T(8,128)(2,1)S(1)} %slice.280), kind=kLoop, calls=%fused_computation.4 | loop fusion | flops 6291456 | bytes 3047424 | tf_op jit(solution)/shard_map/concatenate | solution.py:172
  47.1 2.9 %copy.164 = bf16[32,192,128]{2,1,0:T(8,128)(2,1)} copy(bf16[32,192,128]{1,0,2:T(8,128)(2,1)S(1)} %fusion.1) | data formatting | bytes 3145728 | tf_op jit(solution)/shard_map/concatenate | solution.py:172
  50.0 3.0 %copy.292 = bf16[8,4,2,4,3,8,128]{6,5,4,0,1,3,2:T(8,128)(2,1)} copy(bf16[8,4,2,4,3,8,128]{6,5,4,3,2,1,0:T(8,128)(2,1)} %bitcast.368) | data formatting | bytes 3145728 | tf_op jit(solution)/shard_map/convert_element_type | solution.py:172
  53.1 50.3 %sum_terms.1 = f32[8,3,8,128]{3,2,1,0:T(8,128)} custom-call(bf16[2,4,4,8,3,8,128]{6,5,4,3,2,1,0:T(8,128)(2,1)} %bitcast.369), custom_call_target="tpu_custom_call" | custom-call | tf_op jit(solution)/shard_map/sum_terms/pallas_call | solution.py:145
  103.4 0.7 slice.248
  104.1 1.4 %slice.281 = f32[90,128]{1,0:T(8,128)} slice(f32[192,128]{1,0:T(8,128)} %bitcast.377), slice={[0:90], [0:128]} | slice | bytes 92160 | tf_op jit(solution)/shard_map/slice | solution.py:178
  105.6 1.4 %slice_bitcast_fusion.4 = f32[7680]{0:T(1024)} fusion(f32[192,128]{1,0:T(8,128)} %bitcast.378), kind=kLoop, calls=%fused_computation.211 | loop fusion | bytes 61440 | tf_op jit(solution)/shard_map/reshape | solution.py:179
  113.5 0.8 fusion.112
  114.8 0.7 dynamic-slice_multiply_fusion
  115.5 1.3 %dynamic-slice_multiply_fusion.1 = f32[480]{0:T(512)} fusion(f32[7680]{0:T(1024)} %slice_bitcast_fusion.4, s32[]{:T(128)S(6)} %select_n.7), kind=kLoop, calls=%fused_computation.222 | loop fusion | flops 480 | bytes 3844 | tf_op jit(solution)/shard_map/mul | solution.py:378
  (149 shorter events, 16.7 us)
Async XLA Ops:
  1.6 7.1 %collective-permute-start.1 = (bf16[2,2,1,64,320]{4,3,1,2,0:T(8,128)(2,1)S(1)}, bf16[2,2,1,64,320]{4,3,1,2,0:T(8,128)(2,1)S(1)}, u32[]{:S(2)}, u32[]{:S(2)}) collective-permute-start(bf16[2,2,1,64,320]{4,3,1,2,0:T(8,128)(2,1)S(1)} %pad_maximum_fusion.5), channel_id=1, source_target_pairs={{16,0},{32,16},{48,32},{64,48},{80,64},{96,80},{112,96},{128,112},... | collective-permute-start | bytes 491528 | tf_op jit(solution)/shard_map/ppermute | solution.py:191
  2.9 7.3 %collective-permute-start = (bf16[2,2,1,64,320]{4,3,1,2,0:T(8,128)(2,1)S(1)}, bf16[2,2,1,64,320]{4,3,1,2,0:T(8,128)(2,1)S(1)}, u32[]{:S(2)}, u32[]{:S(2)}) collective-permute-start(bf16[2,2,1,64,320]{4,3,1,2,0:T(8,128)(2,1)S(1)} %pad_maximum_fusion.5), channel_id=1, source_target_pairs={{0,16},{16,32},{32,48},{48,64},{64,80},{80,96},{96,112},{112,128},... | collective-permute-start | bytes 491528 | tf_op jit(solution)/shard_map/ppermute | solution.py:190
  11.3 1.0 copy-start.2
  13.5 1.1 copy-start.18
  13.7 1.0 copy-start.20
  14.7 18.4 %collective-permute-start.3 = (bf16[2,2,1,64,320]{4,3,1,2,0:T(8,128)(2,1)S(1)}, bf16[2,2,1,64,320]{4,3,1,2,0:T(8,128)(2,1)S(1)}, u32[]{:S(2)}, u32[]{:S(2)}) collective-permute-start(bf16[2,2,1,64,320]{4,3,1,2,0:T(8,128)(2,1)S(1)} %pad_maximum_fusion.6), channel_id=1, source_target_pairs={{1,0},{2,1},{3,2},{4,3},{5,4},{6,5},{7,6},{8,7},{9,8},{10,9},{11,1... | collective-permute-start | bytes 491528 | tf_op jit(solution)/shard_map/ppermute | solution.py:191
  26.7 6.4 %collective-permute-start.2 = (bf16[2,2,1,64,320]{4,3,1,2,0:T(8,128)(2,1)S(1)}, bf16[2,2,1,64,320]{4,3,1,2,0:T(8,128)(2,1)S(1)}, u32[]{:S(2)}, u32[]{:S(2)}) collective-permute-start(bf16[2,2,1,64,320]{4,3,1,2,0:T(8,128)(2,1)S(1)} %pad_maximum_fusion.6), channel_id=1, source_target_pairs={{0,1},{1,2},{2,3},{3,4},{4,5},{5,6},{6,7},{7,8},{8,9},{9,10},{10,1... | collective-permute-start | bytes 491528 | tf_op jit(solution)/shard_map/ppermute | solution.py:190
  33.8 2.9 %copy-start.13 = (bf16[2,64,2,160]{3,2,1,0:T(2,128)(2,1)}, bf16[2,64,2,160]{3,2,1,0:T(2,128)(2,1)S(1)}, u32[]{:S(2)}) copy-start(bf16[2,64,2,160]{3,2,1,0:T(2,128)(2,1)S(1)} %reshape.425) | copy-start | bytes 245764
  33.9 2.6 %copy-start.15 = (bf16[2,64,2,160]{3,2,1,0:T(2,128)(2,1)}, bf16[2,64,2,160]{3,2,1,0:T(2,128)(2,1)S(1)}, u32[]{:S(2)}) copy-start(bf16[2,64,2,160]{3,2,1,0:T(2,128)(2,1)S(1)} %reshape.426) | copy-start | bytes 245764
  34.1 2.2 %copy-start.11 = (bf16[2,64,2,160]{3,2,1,0:T(2,128)(2,1)}, bf16[2,64,2,160]{3,2,1,0:T(2,128)(2,1)S(1)}, u32[]{:S(2)}) copy-start(bf16[2,64,2,160]{3,2,1,0:T(2,128)(2,1)S(1)} %reshape.427) | copy-start | bytes 245764
  34.2 1.8 %copy-start.9 = (bf16[2,64,2,160]{3,2,1,0:T(2,128)(2,1)}, bf16[2,64,2,160]{3,2,1,0:T(2,128)(2,1)S(1)}, u32[]{:S(2)}) copy-start(bf16[2,64,2,160]{3,2,1,0:T(2,128)(2,1)S(1)} %reshape.428) | copy-start | bytes 245764
  34.3 1.7 %copy-start.7 = (bf16[2,64,2,160]{3,2,1,0:T(2,128)(2,1)}, bf16[2,64,2,160]{3,2,1,0:T(2,128)(2,1)S(1)}, u32[]{:S(2)}) copy-start(bf16[2,64,2,160]{3,2,1,0:T(2,128)(2,1)S(1)} %reshape.429) | copy-start | bytes 245764
  34.4 1.8 %copy-start.5 = (bf16[2,64,2,160]{3,2,1,0:T(2,128)(2,1)}, bf16[2,64,2,160]{3,2,1,0:T(2,128)(2,1)S(1)}, u32[]{:S(2)}) copy-start(bf16[2,64,2,160]{3,2,1,0:T(2,128)(2,1)S(1)} %reshape.430) | copy-start | bytes 245764
  34.5 1.7 %copy-start.3 = (bf16[2,64,2,160]{3,2,1,0:T(2,128)(2,1)}, bf16[2,64,2,160]{3,2,1,0:T(2,128)(2,1)S(1)}, u32[]{:S(2)}) copy-start(bf16[2,64,2,160]{3,2,1,0:T(2,128)(2,1)S(1)} %reshape.431) | copy-start | bytes 245764
  44.4 1.2 %copy-start.1 = (bf16[32,60,128]{1,0,2:T(8,128)(2,1)S(1)}, bf16[32,60,128]{1,0,2:T(8,128)(2,1)}, u32[]{:S(2)}) copy-start(bf16[32,60,128]{1,0,2:T(8,128)(2,1)} %copy.163) | copy-start | bytes 1474564
  53.0 53.9 %copy-start = (bf16[3,3,2,160,160]{4,3,2,1,0:T(8,128)(2,1)S(1)}, bf16[3,3,2,160,160]{4,3,2,1,0:T(8,128)(2,1)}, u32[]{:S(2)}) copy-start(bf16[3,3,2,160,160]{4,3,2,1,0:T(8,128)(2,1)} %param.10) | copy-start | bytes 2764804
  53.0 53.9 %copy-start.14 = (bf16[2,64,2,160]{3,2,1,0:T(2,128)(2,1)S(1)}, bf16[2,64,2,160]{3,2,1,0:T(2,128)(2,1)}, u32[]{:S(2)}) copy-start(bf16[2,64,2,160]{3,2,1,0:T(2,128)(2,1)} %copy-done.13) | copy-start | bytes 245764
  53.0 54.1 %copy-start.16 = (bf16[2,64,2,160]{3,2,1,0:T(2,128)(2,1)S(1)}, bf16[2,64,2,160]{3,2,1,0:T(2,128)(2,1)}, u32[]{:S(2)}) copy-start(bf16[2,64,2,160]{3,2,1,0:T(2,128)(2,1)} %copy-done.15) | copy-start | bytes 245764
  53.1 54.3 %copy-start.12 = (bf16[2,64,2,160]{3,2,1,0:T(2,128)(2,1)S(1)}, bf16[2,64,2,160]{3,2,1,0:T(2,128)(2,1)}, u32[]{:S(2)}) copy-start(bf16[2,64,2,160]{3,2,1,0:T(2,128)(2,1)} %copy-done.11) | copy-start | bytes 245764
  103.4 4.1 %copy-start.10 = (bf16[2,64,2,160]{3,2,1,0:T(2,128)(2,1)S(1)}, bf16[2,64,2,160]{3,2,1,0:T(2,128)(2,1)}, u32[]{:S(2)}) copy-start(bf16[2,64,2,160]{3,2,1,0:T(2,128)(2,1)} %copy-done.9) | copy-start | bytes 245764
  107.1 0.9 copy-start.6
  107.3 0.9 copy-start.4
  112.6 0.9 copy-start.21
  112.8 1.9 %copy-start.22 = (f32[90,128]{1,0:T(8,128)S(1)}, f32[90,128]{1,0:T(8,128)}, u32[]{:S(2)}) copy-start(f32[90,128]{1,0:T(8,128)} %slice.281) | copy-start | bytes 138244
  (3 other events, 2.7 us)

commit v2 on v1

v2 whole, which is shorter than its diff:
```python
import math

import jax
import jax.numpy as jnp
from jax import lax
from jax.experimental import pallas as pl
from jax.experimental.pallas import tpu as pltpu
from jax.sharding import PartitionSpec as P

MESH = pl.DeviceIdType.MESH
F32, BF16 = jnp.float32, jnp.bfloat16
HAAR = 0.7071067811865476


def place():
    tm, row = lax.axis_index("tm"), lax.axis_index("row")
    return tm // 4, tm % 4, row // 4, (row // 2) % 2, row % 2


def ident(z, yl, x, yh, c):
    return (z * 4 + yl, x * 4 + yh * 2 + c)


def greet(z, yl, x, yh, c):
    peers = []
    for dx in range(4):
        for h in range(2):
            for dc in range(2):
                if dx or h or dc:
                    peers.append(ident(z, yl, (x + dx) % 4, (yh + h) % 2, (c + dc) % 2))
    for j in range(1, 4):
        for h in range(2):
            peers.append(ident(z, (yl + j) % 4, x, (yh + h) % 2, c))
    for d in range(1, 8):
        peers.append(ident((z + d) % 8, yl, x, yh, c))
    barrier = pltpu.get_barrier_semaphore()
    for peer in peers:
        pl.semaphore_signal(barrier, inc=1, device_id=peer, device_id_type=MESH)
    pl.semaphore_wait(barrier, len(peers))


def sum_kernel(p, out, r0, s0, r1, s1, r2, s2, r3, fin, q_snd, q_rcv, x_snd, x_rcv, y_snd, y_rcv, z_snd, z_rcv, g_snd, g_rcv):
    z, yl, x, yh, c = place()
    greet(z, yl, x, yh, c)

    def send(src, dst, snd, rcv, peer):
        return pltpu.make_async_remote_copy(src_ref=src, dst_ref=dst, send_sem=snd, recv_sem=rcv, device_id=peer, device_id_type=MESH)

    started = []
    first = []
    for k in (1, 2, 3, 0):
        xp = (x + k) % 4
        copy = send(p.at[1 - c, xp], r0.at[xp], q_snd.at[k], q_rcv.at[k], ident(z, yl, x, yh, 1 - c))
        copy.start()
        first.append(copy)
    second = {}
    for n, k in enumerate((1, 2, 3, 0)):
        xp = (x + k) % 4
        first[n].wait_recv()
        for j in (1, 2, 3, 0):
            yp = (yl + j) % 4
            s0[xp, yp] = (p[c, xp, yp].astype(F32) + r0[xp, yp].astype(F32)).astype(BF16)
            if k:
                copy = send(s0.at[xp, yp], r1.at[k - 1, yp], x_snd.at[k - 1, j], x_rcv.at[k - 1, j], ident(z, yl, xp, yh, c))
                copy.start()
                second[k, j] = copy
    third = {}
    for j in (1, 2, 3, 0):
        yp = (yl + j) % 4
        for k in (1, 2, 3):
            second[k, j].wait_recv()
        total = s0[x, yp].astype(F32)
        for k in (1, 2, 3):
            total += r1[k - 1, yp].astype(F32)
        s1[yp] = total.astype(BF16)
        for h in (1, 0):
            if j or h:
                hp = (yh + h) % 2
                copy = send(s1.at[yp, pl.ds(hp * 4, 4)], r2.at[2 * j + h], y_snd.at[2 * j + h], y_rcv.at[2 * j + h], ident(z, yp, x, hp, c))
                copy.start()
                third[j, h] = copy
    total = s1[yl, pl.ds(yh * 4, 4)].astype(F32)
    for j, h in third:
        third[j, h].wait_recv()
    for j, h in third:
        total += r2[2 * j + h].astype(F32)
    s2[...] = total.astype(BF16)
    mine = z // 4 == yh
    for d in range(1, 8):
        zp = (z + d) % 8

        @pl.when(zp // 4 == yh)
        def _():
            send(s2.at[zp % 4], r3.at[d - 1], z_snd.at[d - 1], z_rcv.at[d - 1], ident(zp, yl, x, yh, c)).start()

    @pl.when(mine)
    def _():
        for d in range(1, 8):
            send(s2.at[0], r3.at[d - 1], z_snd.at[d - 1], z_rcv.at[d - 1], ident((z + d) % 8, yl, x, yh, c)).wait_recv()
        last = s2[z % 4].astype(F32)
        for d in range(1, 8):
            last += r3[d - 1].astype(F32)
        fin[c * 4 + x] = last
        for dx in range(4):
            for h in range(2):
                for dc in range(2):
                    if dx or h or dc:
                        n = dx * 2 + dc
                        send(fin.at[c * 4 + x], fin.at[c * 4 + x], g_snd.at[n, h], g_rcv.at[n], ident(z, yl, (x + dx) % 4, (yh + h) % 2, (c + dc) % 2)).start()

    for dx in range(4):
        for dc in range(2):
            n = dx * 2 + dc
            src = ((c + dc) % 2) * 4 + (x - dx) % 4

            def wait():
                send(fin.at[src], fin.at[src], g_snd.at[n, 0], g_rcv.at[n], ident(z, yl, (x + dx) % 4, yh, (c + dc) % 2)).wait_recv()

            if n:
                wait()
            else:
                pl.when(jnp.logical_not(mine))(lambda: send(fin.at[src], fin.at[src], g_snd.at[0, 1], g_rcv.at[0], ident(z, yl, x, 1 - yh, c)).wait_recv())
    out[...] = fin[...]
    for copy in first + list(second.values()) + list(third.values()):
        copy.wait_send()
    for d in range(1, 8):
        zp = (z + d) % 8

        @pl.when(zp // 4 == yh)
        def _():
            send(s2.at[zp % 4], r3.at[d - 1], z_snd.at[d - 1], z_rcv.at[d - 1], ident(zp, yl, x, yh, c)).wait_send()

    @pl.when(mine)
    def _():
        for dx in range(4):
            for h in range(2):
                for dc in range(2):
                    if dx or h or dc:
                        n = dx * 2 + dc
                        send(fin.at[c * 4 + x], fin.at[c * 4 + x], g_snd.at[n, h], g_rcv.at[n], ident(z, yl, (x + dx) % 4, (yh + h) % 2, (c + dc) % 2)).wait_send()


def summed(p):
    dma = pltpu.SemaphoreType.DMA
    out = pl.pallas_call(
        sum_kernel,
        out_shape=jax.ShapeDtypeStruct((8, 3, 8, 128), F32),
        in_specs=[pl.BlockSpec(memory_space=pltpu.VMEM)],
        out_specs=pl.BlockSpec(memory_space=pltpu.VMEM),
        scratch_shapes=[
            pltpu.VMEM((4, 4, 8, 3, 8, 128), BF16),
            pltpu.VMEM((4, 4, 8, 3, 8, 128), BF16),
            pltpu.VMEM((3, 4, 8, 3, 8, 128), BF16),
            pltpu.VMEM((4, 8, 3, 8, 128), BF16),
            pltpu.VMEM((8, 4, 3, 8, 128), BF16),
            pltpu.VMEM((4, 3, 8, 128), BF16),
            pltpu.VMEM((7, 3, 8, 128), BF16),
            pltpu.VMEM((8, 3, 8, 128), F32),
            dma((4,)), dma((4,)), dma((3, 4)), dma((3, 4)), dma((8,)), dma((8,)), dma((7,)), dma((7,)), dma((8, 2)), dma((8,)),
        ],
        compiler_params=pltpu.CompilerParams(collective_id=3, has_side_effects=True),
        name="sum_terms",
    )(p)
    return out.reshape(192, 128)


def sigmoid(v):
    return 1.0 / (1.0 + jnp.exp(-v))


def slope(v):
    s = sigmoid(v)
    return s * (1.0 + v * (1.0 - s))


def dot(a, b, ca, cb):
    return lax.dot_general(a, b, (((ca,), (cb,)), ((), ())), preferred_element_type=F32)


def block_kernel(y1, y2, c1, c2, ws, wt, xf, xs, gf, gs, p, tb, hb, sq, cs, wide, pa, pg, sa, rq, g, gt, t_snd, t_rcv, r_snd, r_rcv):
    tm, row = lax.axis_index("tm"), lax.axis_index("row")
    barrier = pltpu.get_barrier_semaphore()
    for peer in (((tm + 1) % 32, row), ((tm + 31) % 32, row), (tm, (row + 1) % 16), (tm, (row + 15) % 16)):
        pl.semaphore_signal(barrier, inc=1, device_id=peer, device_id_type=MESH)

    for n, ref in enumerate((y1, c2)):
        even, odd = ref[0].astype(F32), ref[1].astype(F32)
        sq[n, :, 0:320] = (even + odd) * HAAR
        sq[n, :, 320:640] = (even - odd) * HAAR
    v = sq[0]
    tb[1, 0] = (v * sigmoid(v)).astype(BF16)
    tb[1, 1] = sq[1].astype(BF16)
    zero_t = jnp.zeros((2, 64, 640), BF16)
    zero_r = jnp.zeros((2, 128, 320), BF16)
    first_t, last_t, first_r, last_r = tm == 0, tm == 31, row == 0, row == 15

    def clear(where, ref, slot, zero):
        @pl.when(where)
        def _():
            ref[slot] = zero

    clear(first_t, tb, 0, zero_t)
    clear(last_t, tb, 2, zero_t)
    clear(first_r, hb, 0, zero_r)
    clear(last_r, hb, 2, zero_r)
    pad = jnp.zeros((3, 2, 2, 8, 160), F32)
    for ref in (pa, pg):
        ref[:, :, :, 0:8] = pad
        ref[:, :, :, 72:80] = pad

    pl.semaphore_wait(barrier, 4)

    def swap(ref, snd, rcv, up, down, first, last):
        ahead = pltpu.make_async_remote_copy(src_ref=ref.at[1], dst_ref=ref.at[0], send_sem=snd.at[0], recv_sem=rcv.at[0], device_id=up, device_id_type=MESH)
        behind = pltpu.make_async_remote_copy(src_ref=ref.at[1], dst_ref=ref.at[2], send_sem=snd.at[1], recv_sem=rcv.at[1], device_id=down, device_id_type=MESH)
        has_ahead, has_behind = jnp.logical_not(last), jnp.logical_not(first)

        def start():
            pl.when(has_ahead)(ahead.start)
            pl.when(has_behind)(behind.start)

        def arrive():
            pl.when(has_behind)(ahead.wait_recv)
            pl.when(has_ahead)(behind.wait_recv)

        def sent():
            pl.when(has_ahead)(ahead.wait_send)
            pl.when(has_behind)(behind.wait_send)

        return start, arrive, sent

    t_start, t_arrive, t_sent = swap(tb, t_snd, t_rcv, ((tm + 1) % 32, row), ((tm + 31) % 32, row), first_t, last_t)
    r_start, r_arrive, r_sent = swap(hb, r_snd, r_rcv, (tm, (row + 1) % 16), (tm, (row + 15) % 16), first_r, last_r)
    t_start()

    def time_taps(ks):
        for q in range(5):
            at = pl.ds(q * 128, 128)
            ahead, back = None, None
            for k in ks:
                one = dot(tb[k, 0, :, at], wt[k, q], 1, 0)
                two = dot(tb[2 - k, 1, :, at], wt[k, q], 1, 1)
                ahead, back = (one, two) if ahead is None else (ahead + one, back + two)
            yield at, ahead, back

    def time_terms(ks):
        for k in ks:
            for q in range(5):
                at = pl.ds(q * 128, 128)
                gt[pl.ds((k * 5 + q) * 16, 16)] = dot(tb[1, 0, :, at], tb[2 - k, 1, :, at], 0, 0).reshape(16, 8, 128)

    for at, ahead, back in time_taps((1,)):
        cs[0, :, at] = ahead
        cs[1, :, at] = back
    time_terms((1,))
    t_arrive()
    for at, ahead, back in time_taps((0, 2)):
        cs[0, :, at] = cs[0, :, at] + ahead
        cs[1, :, at] = (cs[1, :, at] + back) * slope(sq[0, :, at])
    for n, (src, out) in enumerate(((y2, xs), (c1, gf))):
        low, high = cs[n, :, 0:320], cs[n, :, 320:640]
        for f in range(2):
            part = ((low + high if f == 0 else low - high) * HAAR).astype(BF16).astype(F32)
            new = (src[f].astype(F32) - part if n == 0 else src[f].astype(F32) + part).astype(BF16)
            out[f] = new
            held = new
            if n == 0:
                w = new.astype(F32)
                held = (w * sigmoid(w)).astype(BF16)
            hb[1, n, pl.ds(f * 64, 64)] = held
    r_start()
    time_terms((0, 2))

    def spread(slot):
        for n, ref in enumerate((pa, pg)):
            wide[n] = hb[slot, n].astype(F32)
            for q in range(2):
                ref[slot, q, :, 8:72] = wide[n, :, pl.ds(q * 160, 160)].reshape(2, 64, 160)

    spread(1)
    for q in range(2):
        rq[q, :, 0:128] = wide[1, :, pl.ds(q * 160, 128)]
        for n in range(4):
            rq[q, :, pl.ds(128 + 32 * n, 32)] = wide[1, :, pl.ds(q * 160 + 128, 32)]

    def space_terms(rows):
        for q in range(2):
            right = rq[q].astype(BF16)
            for a in rows:
                for b in range(3):
                    tap = a * 3 + b
                    left = pa[a, q, :, pl.ds(7 + b, 64)].reshape(128, 160).astype(BF16)
                    sa[tap, q] = left
                    g[pl.ds((tap * 2 + q) * 20, 20)] = dot(left, right, 0, 0).reshape(20, 8, 256)

    def space_taps(rows, q):
        ahead, back = None, None
        for a in rows:
            for b in range(3):
                one = dot(sa[a * 3 + b, q], ws[a, b, q], 1, 0)
                moved = pg[2 - a, q, :, pl.ds(9 - b, 64)].reshape(128, 160).astype(BF16)
                two = dot(moved, ws[a, b, q], 1, 1)
                ahead, back = (one, two) if ahead is None else (ahead + one, back + two)
        return ahead, back

    space_terms((1,))
    r_arrive()
    spread(0)
    spread(2)
    space_terms((0, 2))
    lane = lax.broadcasted_iota(jnp.int32, (3, 8, 128), 2)

    def pack(chunk, carry):
        z, yl = chunk // 4, chunk % 4
        tiles = g[pl.ds((45 * chunk) // 4, 12)]
        for n in range(4):
            p[0, n, yl, z] = tiles[3 * n : 3 * n + 3, :, 0:128].astype(BF16)
        rest = tiles[:, :, 128:256]
        rest = jnp.where(lane < 32, rest[0:3], jnp.where(lane < 64, rest[3:6], jnp.where(lane < 96, rest[6:9], rest[9:12])))
        p[1, 0, yl, z] = rest.astype(BF16)
        tiles = gt[pl.ds((15 * chunk) // 2, 8)]
        p[1, 1, yl, z] = tiles[0:3].astype(BF16)
        p[1, 2, yl, z] = tiles[3:6].astype(BF16)
        p[1, 3, yl, z, 0:2] = tiles[6:8].astype(BF16)
        p[1, 3, yl, z, 2:3] = jnp.zeros((1, 8, 128), BF16)
        return carry

    lax.fori_loop(0, 32, pack, 0)
    for q in range(2):
        ahead, back = space_taps((0, 1, 2), q)
        wide[0, :, pl.ds(q * 160, 160)] = ahead
        wide[1, :, pl.ds(q * 160, 160)] = back
    for f in range(2):
        at = pl.ds(f * 64, 64)
        xf[f] = (y1[f].astype(F32) - wide[0, at]).astype(BF16)
        gs[f] = (c2[f].astype(F32) + wide[1, at] * slope(xs[f].astype(F32))).astype(BF16)
    t_sent()
    r_sent()


def block(y1, y2, c1, c2, ws, wt):
    dma = pltpu.SemaphoreType.DMA
    here = pl.BlockSpec(memory_space=pltpu.VMEM)
    one = jax.ShapeDtypeStruct((2, 64, 320), BF16)
    return pl.pallas_call(
        block_kernel,
        out_shape=[one] * 4 + [jax.ShapeDtypeStruct((2, 4, 4, 8, 3, 8, 128), BF16)],
        in_specs=[here] * 6,
        out_specs=[here] * 5,
        scratch_shapes=[
            pltpu.VMEM((3, 2, 64, 640), BF16),
            pltpu.VMEM((3, 2, 128, 320), BF16),
            pltpu.VMEM((2, 64, 640), F32),
            pltpu.VMEM((2, 64, 640), F32),
            pltpu.VMEM((2, 128, 320), F32),
            pltpu.VMEM((3, 2, 2, 80, 160), F32),
            pltpu.VMEM((3, 2, 2, 80, 160), F32),
            pltpu.VMEM((9, 2, 128, 160), BF16),
            pltpu.VMEM((2, 128, 256), F32),
            pltpu.VMEM((360, 8, 256), F32),
            pltpu.VMEM((240, 8, 128), F32),
            dma((2,)), dma((2,)), dma((2,)), dma((2,)),
        ],
        compiler_params=pltpu.CompilerParams(collective_id=5, has_side_effects=True, vmem_limit_bytes=40 * 1024 * 1024),
        name="block",
    )(y1, y2, c1, c2, ws, wt)


def shares(chunk, tm, row):
    rest = chunk[96:120].reshape(24, 4, 32).transpose(1, 0, 2).reshape(96, 32)
    space = jnp.concatenate([chunk[:96], rest], axis=1).reshape(-1)
    time = chunk[120:184].reshape(-1)
    return (
        lax.dynamic_slice(space, (90 * tm % 8 * 160 + 900 * row,), (900,)),
        lax.dynamic_slice(time, (60 * tm % 8 * 128 + 480 * row,), (480,)),
    )


def per_device(output_first_half, y_second, cot_first, cot_second, weight_space, temporal_weight):
    cells_all = output_first_half.shape[0] * output_first_half.shape[1] * output_first_half.shape[2] * lax.axis_size("tm") * lax.axis_size("row")
    factor = 1.0 / math.sqrt(cells_all)
    flat = [v.reshape(2, 64, 320) for v in (output_first_half, y_second, cot_first, cot_second)]
    *outs, p = block(*flat, weight_space, temporal_weight)
    chunk = summed(p)
    space_share, time_share = shares(chunk, lax.axis_index("tm"), lax.axis_index("row"))
    return tuple(v.reshape(output_first_half.shape) for v in outs) + (space_share * factor, time_share * factor)


def solution(mesh):
    in_specs = (
        P("tm", "row", None, None),
        P("tm", "row", None, None),
        P("tm", "row", None, None),
        P("tm", "row", None, None),
        P(),
        P(),
    )
    out_specs = (
        P("tm", "row", None, None),
        P("tm", "row", None, None),
        P("tm", "row", None, None),
        P("tm", "row", None, None),
        P(("tm", "row")),
        P(("tm", "row")),
    )
    return jax.shard_map(
        per_device, mesh=mesh, in_specs=in_specs, out_specs=out_specs, check_vma=False
    )
```

time: 118 us -> 86.6 us (0.73)
  the two profiles are of different devices: /device:TPU:1 before, /device:TPU:49 now
where the time goes in v2:
time: 86.6 us; the launch traced here: 86 us
  Pallas kernels  71.8 us (83%)
  local copies, waits for them, and re-layouts  12.1 us (14%)
  other arithmetic  1.34 us (2%)
    pallas_call x1, Pallas kernels, summed(): pl.pallas_call(sum_kernel, out_shape=jax.ShapeDtypeStruct((8, 3, 8, 128),...  45.2 us
    pallas_call x1, Pallas kernels, block(): pl.pallas_call(block_kernel, out_shape=[one] * 4 + [jax.ShapeDtypeStruct(...  26.6 us
    unnamed x18, local copies, waits for them, and re-layouts  9.66 us

profile of v2, /device:TPU:49, one launch (start us, length us, event | category | flops | bytes accessed | tf_op | source)
XLA Modules:
  0.0 86.0 jit_solution(4547148906812845168)
XLA Ops:
  0.6 0.0 copy-start.1
  0.6 1.4 %copy-done.1 = bf16[3,3,2,160,160]{4,3,2,1,0:T(8,128)(2,1)S(1)} copy-done((bf16[3,3,2,160,160]{4,3,2,1,0:T(8,128)(2,1)S(1)}, bf16[3,3,2,160,160]{4,3,2,1,0:T(8,128)(2,1)}, u32[]{:S(2)}) %copy-start.1) | copy-done | bytes 921624
  2.0 0.0 copy-start.2
  2.0 1.0 %copy-done.2 = bf16[3,5,128,128]{3,2,1,0:T(8,128)(2,1)S(1)} copy-done((bf16[3,5,128,128]{3,2,1,0:T(8,128)(2,1)S(1)}, bf16[3,5,128,128]{3,2,1,0:T(8,128)(2,1)}, u32[]{:S(2)}) %copy-start.2) | copy-done | bytes 491544
  3.0 0.0 copy-start.3
  3.0 0.9 %copy-done.3 = bf16[2,1,64,320]{3,2,1,0:T(8,128)(2,1)S(1)} copy-done((bf16[2,1,64,320]{3,2,1,0:T(8,128)(2,1)S(1)}, bf16[2,1,64,320]{3,2,1,0:T(8,128)(2,1)}, u32[]{:S(2)}) %copy-start.3) | copy-done | bytes 81944
  3.9 0.9 %copy-done.4 = bf16[2,1,64,320]{3,2,1,0:T(8,128)(2,1)S(1)} copy-done((bf16[2,1,64,320]{3,2,1,0:T(8,128)(2,1)S(1)}, bf16[2,1,64,320]{3,2,1,0:T(8,128)(2,1)}, u32[]{:S(2)}) %copy-start.4) | copy-done | bytes 81944
  4.8 0.9 %copy-done.5 = bf16[2,1,64,320]{3,2,1,0:T(8,128)(2,1)S(1)} copy-done((bf16[2,1,64,320]{3,2,1,0:T(8,128)(2,1)S(1)}, bf16[2,1,64,320]{3,2,1,0:T(8,128)(2,1)}, u32[]{:S(2)}) %copy-start.5) | copy-done | bytes 81944
  5.7 0.9 %copy-done.6 = bf16[2,1,64,320]{3,2,1,0:T(8,128)(2,1)S(1)} copy-done((bf16[2,1,64,320]{3,2,1,0:T(8,128)(2,1)S(1)}, bf16[2,1,64,320]{3,2,1,0:T(8,128)(2,1)}, u32[]{:S(2)}) %copy-start.6) | copy-done | bytes 81944
  6.6 26.6 %block.1 = (bf16[2,64,320]{2,1,0:T(8,128)(2,1)S(1)}, bf16[2,64,320]{2,1,0:T(8,128)(2,1)S(1)}, bf16[2,64,320]{2,1,0:T(8,128)(2,1)S(1)}, bf16[2,64,320]{2,1,0:T(8,...) custom-call(bf16[2,64,320]{2,1,0:T(8,128)(2,1)S(1)} %bitcast.25, bf16[2,64,320]{2,1,0:T(8,128)(2,1)S(1)} %bitcast.26, ...), custom_call_target="tpu_custom_call" | custom-call | tf_op jit(solution)/shard_map/block/pallas_call | solution.py:345
  33.3 0.0 copy-start
  33.3 1.1 %copy-done = bf16[2,4,4,8,3,8,128]{6,5,4,3,2,1,0:T(8,128)(2,1)} copy-done((bf16[2,4,4,8,3,8,128]{6,5,4,3,2,1,0:T(8,128)(2,1)}, bf16[2,4,4,8,3,8,128]{6,5,4,3,2,1,0:T(8,128)(2,1)S(1)}, u32[]{:S(2)}) %copy-start) | copy-done | bytes 1572888
  34.4 45.2 %sum_terms.1 = f32[8,3,8,128]{3,2,1,0:T(8,128)} custom-call(bf16[2,4,4,8,3,8,128]{6,5,4,3,2,1,0:T(8,128)(2,1)} %copy-done), custom_call_target="tpu_custom_call" | custom-call | tf_op jit(solution)/shard_map/sum_terms/pallas_call | solution.py:145
  79.6 0.7 slice.15
  80.3 0.1 reshape.62
  80.4 0.8 slice.13
  81.2 0.1 reshape.64
  81.4 0.7 dynamic-slice_multiply_fusion
  82.1 0.8 slice_bitcast_fusion
  82.8 0.7 dynamic-slice_multiply_fusion.1
  83.5 0.6 copy.28
  84.1 0.6 copy.29
  84.7 0.6 copy.30
  85.4 0.6 copy.31
  (5 shorter events, 0.0 us)
Async XLA Ops:
  0.6 1.4 %copy-start.1 = (bf16[3,3,2,160,160]{4,3,2,1,0:T(8,128)(2,1)S(1)}, bf16[3,3,2,160,160]{4,3,2,1,0:T(8,128)(2,1)}, u32[]{:S(2)}) copy-start(bf16[3,3,2,160,160]{4,3,2,1,0:T(8,128)(2,1)} %ws.1) | copy-start | bytes 2764804
  2.0 1.0 %copy-start.2 = (bf16[3,5,128,128]{3,2,1,0:T(8,128)(2,1)S(1)}, bf16[3,5,128,128]{3,2,1,0:T(8,128)(2,1)}, u32[]{:S(2)}) copy-start(bf16[3,5,128,128]{3,2,1,0:T(8,128)(2,1)} %wt.1) | copy-start | bytes 1474564
  3.0 0.9 %copy-start.3 = (bf16[2,1,64,320]{3,2,1,0:T(8,128)(2,1)S(1)}, bf16[2,1,64,320]{3,2,1,0:T(8,128)(2,1)}, u32[]{:S(2)}) copy-start(bf16[2,1,64,320]{3,2,1,0:T(8,128)(2,1)} %param.6) | copy-start | bytes 245764
  3.9 0.9 %copy-start.4 = (bf16[2,1,64,320]{3,2,1,0:T(8,128)(2,1)S(1)}, bf16[2,1,64,320]{3,2,1,0:T(8,128)(2,1)}, u32[]{:S(2)}) copy-start(bf16[2,1,64,320]{3,2,1,0:T(8,128)(2,1)} %param.7) | copy-start | bytes 245764
  4.8 0.9 %copy-start.5 = (bf16[2,1,64,320]{3,2,1,0:T(8,128)(2,1)S(1)}, bf16[2,1,64,320]{3,2,1,0:T(8,128)(2,1)}, u32[]{:S(2)}) copy-start(bf16[2,1,64,320]{3,2,1,0:T(8,128)(2,1)} %param.8) | copy-start | bytes 245764
  5.7 0.9 %copy-start.6 = (bf16[2,1,64,320]{3,2,1,0:T(8,128)(2,1)S(1)}, bf16[2,1,64,320]{3,2,1,0:T(8,128)(2,1)}, u32[]{:S(2)}) copy-start(bf16[2,1,64,320]{3,2,1,0:T(8,128)(2,1)} %param.9) | copy-start | bytes 245764
  33.3 1.1 %copy-start = (bf16[2,4,4,8,3,8,128]{6,5,4,3,2,1,0:T(8,128)(2,1)}, bf16[2,4,4,8,3,8,128]{6,5,4,3,2,1,0:T(8,128)(2,1)S(1)}, u32[]{:S(2)}) copy-start(bf16[2,4,4,8,3,8,128]{6,5,4,3,2,1,0:T(8,128)(2,1)S(1)} %get-tuple-element.15.p) | copy-start | bytes 4718596

commit v3 on v0

v3 whole, which is shorter than its diff:
```python
import math

import jax
import jax.numpy as jnp
from jax import lax
from jax.experimental import pallas as pl
from jax.experimental.pallas import tpu as pltpu
from jax.sharding import PartitionSpec as P

MESH = pl.DeviceIdType.MESH
F32, BF16 = jnp.float32, jnp.bfloat16
HAAR = 0.7071067811865476
SHIFT, EARLY = 5, 2


def place():
    tm, row = lax.axis_index("tm"), lax.axis_index("row")
    return tm // 4, tm % 4, row // 4, (row // 2) % 2, row % 2


def ident(z, yl, x, yh, c):
    return (z * 4 + yl, x * 4 + yh * 2 + c)


def sigmoid(v):
    return 1.0 / (1.0 + jnp.exp(-v))


def slope(v):
    s = sigmoid(v)
    return s * (1.0 + v * (1.0 - s))


def dot(a, b, ca, cb):
    return lax.dot_general(a, b, (((ca,), (cb,)), ((), ())), preferred_element_type=F32)


def send(src, dst, snd, rcv, peer):
    return pltpu.make_async_remote_copy(
        src_ref=src, dst_ref=dst, send_sem=snd, recv_sem=rcv, device_id=peer, device_id_type=MESH
    )


def greet(z, yl, x, yh, c):
    tm, row = z * 4 + yl, x * 4 + yh * 2 + c
    peers = [((tm + 1) % 32, row), ((tm + 31) % 32, row), (tm, (row + 2 * c + 15) % 16)]
    for dx in range(4):
        for h in range(2):
            for dc in range(2):
                if dx or h or dc:
                    peers.append(ident(z, yl, (x + dx) % 4, (yh + h) % 2, (c + dc) % 2))
    for j in range(1, 4):
        for h in range(2):
            peers.append(ident(z, (yl + j) % 4, x, (yh + h) % 2, c))
    for d in range(1, 8):
        peers.append(ident((z + d) % 8, yl, x, yh, c))
    barrier = pltpu.get_barrier_semaphore()
    for peer in peers:
        pl.semaphore_signal(barrier, inc=1, device_id=peer, device_id_type=MESH)
    return barrier, len(peers)


def block_kernel(
    y1h, y2h, c1h, c2h, wsh, wth, xf, xs, gf, gs, out,
    y1, y2, c1, c2, ws, wt, tb, hb, sq, cs, wide, pa, pg, sa, rq, g, gt, rt, s0, r1, s1, r2, s2, r3, fin,
    in_sem, t_snd, t_rcv, n_snd, n_rcv, r_snd, r_rcv, f_snd, f_rcv, q_snd, q_rcv, x_snd, x_rcv, y_snd, y_rcv, z_snd, z_rcv, g_snd, g_rcv,
):
    z, yl, x, yh, c = place()
    tm, row = z * 4 + yl, x * 4 + yh * 2 + c
    loads = [
        pltpu.make_async_copy(src, dst, in_sem.at[n])
        for n, (src, dst) in enumerate(((y1h, y1), (c2h, c2), (wth, wt), (y2h, y2), (c1h, c1), (wsh, ws)))
    ]
    for load in loads:
        load.start()
    barrier, met = greet(z, yl, x, yh, c)
    partner = ident(z, yl, x, yh, 1 - c)
    first_t, last_t = tm == 0, tm == 31
    own, other, far = 1 + c, 2 - c, 3 * c
    has_far = jnp.logical_not(jnp.logical_or(row == 0, row == 15))
    pad = jnp.zeros((4, 2, 2, 8, 160), F32)
    for ref in (pa, pg):
        ref[:, :, :, 0:8] = pad
        ref[:, :, :, 72:80] = pad

    @pl.when(first_t)
    def _():
        tb[0] = jnp.zeros((2, 64, 640), BF16)

    @pl.when(last_t)
    def _():
        tb[2] = jnp.zeros((2, 64, 640), BF16)

    @pl.when(jnp.logical_not(has_far))
    def _():
        hb[far] = jnp.zeros((2, 128, 320), BF16)

    for n, ref in enumerate((y1, c2)):
        loads[n].wait()
        even, odd = ref[0].astype(F32), ref[1].astype(F32)
        sq[n, :, 0:320] = (even + odd) * HAAR
        sq[n, :, 320:640] = (even - odd) * HAAR
    v = sq[0]
    tb[1, 0] = (v * sigmoid(v)).astype(BF16)
    tb[1, 1] = sq[1].astype(BF16)
    pl.semaphore_wait(barrier, met)

    ahead_t = send(tb.at[1], tb.at[0], t_snd.at[0], t_rcv.at[0], ((tm + 1) % 32, row))
    behind_t = send(tb.at[1], tb.at[2], t_snd.at[1], t_rcv.at[1], ((tm + 31) % 32, row))
    has_next, has_last = jnp.logical_not(last_t), jnp.logical_not(first_t)
    pl.when(has_next)(ahead_t.start)
    pl.when(has_last)(behind_t.start)

    def time_taps(ks):
        for q in range(5):
            at = pl.ds(q * 128, 128)
            ahead, back = None, None
            for k in ks:
                one = dot(tb[k, 0, :, at], wt[k, q], 1, 0)
                two = dot(tb[2 - k, 1, :, at], wt[k, q], 1, 1)
                ahead, back = (one, two) if ahead is None else (ahead + one, back + two)
            yield at, ahead, back

    def time_terms(ks):
        for k in ks:
            for q in range(5):
                at = pl.ds(q * 128, 128)
                gt[pl.ds((k * 5 + q) * 16, 16)] = dot(tb[1, 0, :, at], tb[2 - k, 1, :, at], 0, 0).reshape(16, 8, 128)

    loads[2].wait()
    for at, ahead, back in time_taps((1,)):
        cs[0, :, at] = ahead
        cs[1, :, at] = back
    time_terms((1,))
    loads[3].wait()
    loads[4].wait()
    pl.when(has_last)(ahead_t.wait_recv)
    pl.when(has_next)(behind_t.wait_recv)
    for at, ahead, back in time_taps((0, 2)):
        cs[0, :, at] = cs[0, :, at] + ahead
        cs[1, :, at] = (cs[1, :, at] + back) * slope(sq[0, :, at])
    for n, (src, res) in enumerate(((y2, xs), (c1, gf))):
        low, high = cs[n, :, 0:320], cs[n, :, 320:640]
        for f in range(2):
            part = ((low + high if f == 0 else low - high) * HAAR).astype(BF16).astype(F32)
            new = (src[f].astype(F32) - part if n == 0 else src[f].astype(F32) + part).astype(BF16)
            res[f] = new
            held = new
            if n == 0:
                w = new.astype(F32)
                held = (w * sigmoid(w)).astype(BF16)
            hb[own, n, pl.ds(f * 64, 64)] = held
    far_row = send(hb.at[own], hb.at[3 - far], r_snd.at[0], r_rcv.at[0], (tm, (row + 2 * c + 15) % 16))
    pl.when(has_far)(far_row.start)
    near_row = send(hb.at[own], hb.at[own], n_snd.at[0], n_rcv.at[0], partner)
    near_row.start()

    time_terms((0, 2))

    def pack_time(n, carry):
        chunk = (n // 4 + 8 - SHIFT) % 8 * 4 + n % 4
        tiles = gt[pl.ds((15 * chunk) // 2, 8)].astype(BF16)

        def put(ref, m):
            ref[m, n % 4, n // 4] = tiles[0:3]
            ref[m + 1, n % 4, n // 4] = tiles[3:6]
            ref[m + 2, n % 4, n // 4, 0:2] = tiles[6:8]
            ref[m + 2, n % 4, n // 4, 2:3] = jnp.zeros((1, 8, 128), BF16)

        pl.when(c == 0)(lambda: put(rt, 0))
        pl.when(c == 1)(lambda: put(s0, 1))
        return carry

    lax.fori_loop(0, 32, pack_time, 0)
    time_half = [send(rt.at[xp - 1], rt.at[xp - 1], q_snd.at[xp - 1], q_rcv.at[xp - 1], partner) for xp in (1, 2, 3)]

    @pl.when(c == 0)
    def _():
        for copy in time_half:
            copy.start()

    def spread(slot):
        for n, ref in enumerate((pa, pg)):
            wide[n] = hb[slot, n].astype(F32)
            for q in range(2):
                ref[slot, q, :, 8:72] = wide[n, :, pl.ds(q * 160, 160)].reshape(2, 64, 160)

    def right_side(slot):
        for q in range(2):
            for n in range(4):
                rq[q, slot - 1, :, pl.ds(32 * n, 32)] = jnp.where(
                    c == 0, wide[1, :, pl.ds(q * 160 + 32 * n, 32)], wide[1, :, pl.ds(q * 160 + 128, 32)]
                ).astype(BF16)

    spread(own)
    near_row.wait_recv()
    spread(other)
    for slot in (1, 2):
        wide[1] = hb[slot, 1].astype(F32)
        right_side(slot)

    def left(slot, b, q):
        return pa[slot, q, :, pl.ds(7 + b, 64)].reshape(128, 160).astype(BF16)

    def space_terms(rows):
        for q in range(2):
            for a in rows:
                for b in range(3):
                    tap = a * 3 + b
                    both = jnp.concatenate([left(a, b, q), left(a + 1, b, q)], axis=0)
                    g[pl.ds((tap * 2 + q) * 20, 20)] = dot(both, rq[q].reshape(256, 128), 0, 0).reshape(20, 8, 128)

    lane = lax.broadcasted_iota(jnp.int32, (3, 8, 128), 2)

    def pack_space(lo, hi):
        def pack(n, carry):
            zz, yp = n // 4, n % 4
            chunk = (zz + 8 - SHIFT) % 8 * 4 + yp
            tiles = g[pl.ds((45 * chunk) // 4, 12)]

            @pl.when(c == 0)
            def _():
                for m in range(4):
                    s0[m, yp, zz] = tiles[3 * m : 3 * m + 3].astype(BF16)

            @pl.when(c == 1)
            def _():
                one, two = jnp.where(lane < 32, tiles[0:3], tiles[3:6]), jnp.where(lane < 96, tiles[6:9], tiles[9:12])
                s0[0, yp, zz] = jnp.where(lane < 64, one, two).astype(BF16)

            return carry

        lax.fori_loop(lo * 4, hi * 4, pack, 0)

    def along_x(k, j, part):
        xp, yp = (x + k) % 4, (yl + j) % 4
        at = pl.ds(0, EARLY) if part == 0 else pl.ds(EARLY, 8 - EARLY)
        return send(s0.at[xp, yp, at], r1.at[k - 1, yp, at], x_snd.at[k - 1, j, part], x_rcv.at[k - 1, j, part], ident(z, yl, xp, yh, c))

    space_terms((1,))

    @pl.when(c == 1)
    def _():
        for xp in (1, 2, 3):
            time_half[xp - 1].wait_recv()
            for yp in range(4):
                s0[xp, yp] = (s0[xp, yp].astype(F32) + rt[xp - 1, yp].astype(F32)).astype(BF16)

    pack_space(0, EARLY)
    timed = [jnp.logical_and(c == 1, (x + k) % 4 != 0) for k in range(4)]
    for k in (1, 2, 3):
        for j in (1, 2, 3, 0):
            along_x(k, j, 0).start()
            pl.when(timed[k])(along_x(k, j, 1).start)

    pl.when(has_far)(far_row.wait_recv)
    pass_on = send(hb.at[far, 0], hb.at[far, 0], f_snd.at[0], f_rcv.at[0], partner)
    pass_on.start()
    spread(far)
    for q in range(2):
        ahead, back = None, None
        for a in range(3):
            for b in range(3):
                moved = left(c + a, b, q)
                one = dot(moved, ws_at(ws, loads, a, b, q), 1, 0)
                moved = pg[c + 2 - a, q, :, pl.ds(9 - b, 64)].reshape(128, 160).astype(BF16)
                two = dot(moved, ws[a, b, q], 1, 1)
                ahead, back = (one, two) if ahead is None else (ahead + one, back + two)
        sa[0, :, pl.ds(q * 160, 160)] = ahead
        sa[1, :, pl.ds(q * 160, 160)] = back
    pass_on.wait_recv()
    wide[0] = hb[3 - far, 0].astype(F32)
    for q in range(2):
        pa[3 - far, q, :, 8:72] = wide[0, :, pl.ds(q * 160, 160)].reshape(2, 64, 160)
    space_terms((0, 2))
    pack_space(EARLY, 8)
    for k in (1, 2, 3):
        for j in (1, 2, 3, 0):
            pl.when(jnp.logical_not(timed[k]))(along_x(k, j, 1).start)
    for f in range(2):
        at = pl.ds(f * 64, 64)
        xf[f] = (y1[f].astype(F32) - sa[0, at]).astype(BF16)
        gs[f] = (c2[f].astype(F32) + sa[1, at] * slope(xs[f].astype(F32))).astype(BF16)

    third = {}
    for j in (1, 2, 3, 0):
        yp = (yl + j) % 4
        for k in (1, 2, 3):
            for part in range(2):
                along_x(k, j, part).wait_recv()
        total = s0[x, yp].astype(F32)
        for k in (1, 2, 3):
            total += r1[k - 1, yp].astype(F32)
        s1[yp] = total.astype(BF16)
        for h in (1, 0):
            if j or h:
                hp = (yh + h) % 2
                copy = send(s1.at[yp, pl.ds(hp * 4, 4)], r2.at[2 * j + h], y_snd.at[2 * j + h], y_rcv.at[2 * j + h], ident(z, yp, x, hp, c))
                copy.start()
                third[j, h] = copy
    total = s1[yl, pl.ds(yh * 4, 4)].astype(F32)
    for j, h in third:
        third[j, h].wait_recv()
    for j, h in third:
        total += r2[2 * j + h].astype(F32)
    s2[...] = total.astype(BF16)

    mine = (z + SHIFT) % 8 // 4 == yh

    def along_z(d, finish):
        zp = (z + d) % 8
        zz = (zp + SHIFT) % 8
        copy = send(s2.at[zz % 4], r3.at[d - 1], z_snd.at[d - 1], z_rcv.at[d - 1], ident(zp, yl, x, yh, c))
        pl.when(zz // 4 == yh)(copy.wait_send if finish else copy.start)

    def over_row(finish):
        for dx in range(4):
            for h in range(2):
                for dc in range(2):
                    if dx or h or dc:
                        n = dx * 2 + dc
                        copy = send(fin.at[c * 4 + x], fin.at[c * 4 + x], g_snd.at[n, h], g_rcv.at[n], ident(z, yl, (x + dx) % 4, (yh + h) % 2, (c + dc) % 2))
                        copy.wait_send() if finish else copy.start()

    for d in range(1, 8):
        along_z(d, False)

    @pl.when(mine)
    def _():
        for d in range(1, 8):
            send(s2.at[0], r3.at[d - 1], z_snd.at[d - 1], z_rcv.at[d - 1], ident((z + d) % 8, yl, x, yh, c)).wait_recv()
        last = s2[(z + SHIFT) % 4].astype(F32)
        for d in range(1, 8):
            last += r3[d - 1].astype(F32)
        fin[c * 4 + x] = last
        over_row(False)

    pl.when(has_next)(ahead_t.wait_send)
    pl.when(has_last)(behind_t.wait_send)
    pl.when(has_far)(far_row.wait_send)
    near_row.wait_send()
    pass_on.wait_send()

    @pl.when(c == 0)
    def _():
        for copy in time_half:
            copy.wait_send()

    for k in (1, 2, 3):
        for j in range(4):
            for part in range(2):
                along_x(k, j, part).wait_send()
    for copy in third.values():
        copy.wait_send()
    for d in range(1, 8):
        along_z(d, True)

    for dx in range(4):
        for dc in range(2):
            n = dx * 2 + dc
            src = (c + dc) % 2 * 4 + (x - dx) % 4
            copy = send(fin.at[src], fin.at[src], g_snd.at[n, 1], g_rcv.at[n], ident(z, yl, (x + dx) % 4, 1 - yh, (c + dc) % 2))
            if n:
                copy.wait_recv()
            else:
                pl.when(jnp.logical_not(mine))(copy.wait_recv)
    out[...] = fin[...]
    pl.when(mine)(lambda: over_row(True))


def ws_at(ws, loads, a, b, q):
    if (a, b, q) == (0, 0, 0):
        loads[5].wait()
    return ws[a, b, q]


def block(y1, y2, c1, c2, ws, wt):
    dma = pltpu.SemaphoreType.DMA
    here, there = pl.BlockSpec(memory_space=pltpu.VMEM), pl.BlockSpec(memory_space=pl.ANY)
    one = jax.ShapeDtypeStruct((2, 64, 320), BF16)
    vm = pltpu.VMEM
    return pl.pallas_call(
        block_kernel,
        out_shape=[one] * 4 + [jax.ShapeDtypeStruct((8, 3, 8, 128), F32)],
        in_specs=[there] * 6,
        out_specs=[here] * 5,
        scratch_shapes=[vm((2, 64, 320), BF16)] * 4
        + [
            vm((3, 3, 2, 160, 160), BF16),
            vm((3, 5, 128, 128), BF16),
            vm((3, 2, 64, 640), BF16),
            vm((4, 2, 128, 320), BF16),
            vm((2, 64, 640), F32),
            vm((2, 64, 640), F32),
            vm((2, 128, 320), F32),
            vm((4, 2, 2, 80, 160), F32),
            vm((4, 2, 2, 80, 160), F32),
            vm((2, 128, 320), F32),
            vm((2, 2, 128, 128), BF16),
            vm((360, 8, 128), F32),
            vm((240, 8, 128), F32),
            vm((3, 4, 8, 3, 8, 128), BF16),
            vm((4, 4, 8, 3, 8, 128), BF16),
            vm((3, 4, 8, 3, 8, 128), BF16),
            vm((4, 8, 3, 8, 128), BF16),
            vm((8, 4, 3, 8, 128), BF16),
            vm((4, 3, 8, 128), BF16),
            vm((7, 3, 8, 128), BF16),
            vm((8, 3, 8, 128), F32),
        ]
        + [dma((6,))]
        + [dma((2,))] * 2
        + [dma((1,))] * 6
        + [dma((3,))] * 2
        + [dma((3, 4, 2))] * 2
        + [dma((8,))] * 2
        + [dma((7,))] * 2
        + [dma((8, 2)), dma((8,))],
        compiler_params=pltpu.CompilerParams(collective_id=5, has_side_effects=True, vmem_limit_bytes=60 * 1024 * 1024),
        name="block",
    )(y1, y2, c1, c2, ws, wt)


def tail_kernel(factor, xf, xs, gf, gs, chunk, xf_o, xs_o, gf_o, gs_o, space, time, rest, line):
    tm, row = lax.axis_index("tm"), lax.axis_index("row")
    for src, dst in ((xf, xf_o), (xs, xs_o), (gf, gf_o), (gs, gs_o)):
        dst[...] = src[...]
    four = chunk[4].reshape(24, 128)
    for n in range(4):
        rest[pl.ds(24 * n, 24), 0:32] = four[:, 32 * n : 32 * n + 32]
    flat = 900 * row
    start = 90 * tm % 8 + flat // 160
    main = pltpu.roll(chunk[0:4].reshape(96, 128), (96 - start) % 96, 0)
    side = pltpu.roll(rest[...], (96 - start) % 96, 0)
    for n in range(7):
        line[0:1, pl.ds(160 * n, 128)] = main[n : n + 1]
        line[0:1, pl.ds(160 * n + 128, 32)] = side[n : n + 1, 0:32]
    space[...] = pltpu.roll(line[...], (1280 - flat % 160) % 1280, 1)[0:1, 0:900] * factor
    flat = 480 * row
    start = 60 * tm % 8 + flat // 128
    main = pltpu.roll(chunk[5:8].reshape(72, 128), (72 - start) % 72, 0)
    for n in range(5):
        line[0:1, pl.ds(128 * n, 128)] = main[n : n + 1]
    time[...] = pltpu.roll(line[...], (1280 - flat % 128) % 1280, 1)[0:1, 0:480] * factor


def tail(factor, outs, chunk):
    here = pl.BlockSpec(memory_space=pltpu.VMEM)
    one = jax.ShapeDtypeStruct((2, 64, 320), BF16)
    return pl.pallas_call(
        lambda *refs: tail_kernel(factor, *refs),
        out_shape=[one] * 4 + [jax.ShapeDtypeStruct((1, 900), F32), jax.ShapeDtypeStruct((1, 480), F32)],
        in_specs=[here] * 5,
        out_specs=[here] * 6,
        scratch_shapes=[pltpu.VMEM((96, 128), F32), pltpu.VMEM((8, 1280), F32)],
        name="tail",
    )(*outs, chunk)


def per_device(output_first_half, y_second, cot_first, cot_second, weight_space, temporal_weight):
    cells_all = (
        output_first_half.shape[0]
        * output_first_half.shape[1]
        * output_first_half.shape[2]
        * lax.axis_size("tm")
        * lax.axis_size("row")
    )
    factor = 1.0 / math.sqrt(cells_all)
    flat = [v.reshape(2, 64, 320) for v in (output_first_half, y_second, cot_first, cot_second)]
    *outs, chunk = block(*flat, weight_space, temporal_weight)
    *outs, space, time = tail(factor, outs, chunk)
    return tuple(v.reshape(output_first_half.shape) for v in outs) + (space.reshape(-1), time.reshape(-1))


def solution(mesh):
    in_specs = (
        P("tm", "row", None, None),
        P("tm", "row", None, None),
        P("tm", "row", None, None),
        P("tm", "row", None, None),
        P(),
        P(),
    )
    out_specs = (
        P("tm", "row", None, None),
        P("tm", "row", None, None),
        P("tm", "row", None, None),
        P("tm", "row", None, None),
        P(("tm", "row")),
        P(("tm", "row")),
    )
    return jax.shard_map(
        per_device, mesh=mesh, in_specs=in_specs, out_specs=out_specs, check_vma=False
    )
```

time: 375 us -> 66.2 us (0.18)
  waiting for transfers between devices: 293 us -> 0 us
  Pallas kernels: 0 us -> 65.4 us
  matrix products: 20.4 us -> 0 us
  starting transfers between devices: 19.9 us -> 0 us
  local copies, waits for them, and re-layouts: 16.5 us -> 0 us
  between operations: 14.7 us -> 0.64 us
  other arithmetic: 9.74 us -> 0 us
    unnamed x2 -> x0, waiting for transfers between devices: 290 us -> none
    pallas_call x0 -> x2, Pallas kernels: none -> 65.4 us  [the longest x1 63.4 us: block(): pl.pallas_call(block_kernel, out_shape=[one] * 4 + [jax.ShapeDtypeStruct(...]
    dot_general x36 -> x0, matrix products: 20.4 us -> none  [the longest x9 9.76 us: space_apply(): jnp.einsum('...gi,gio->...go', window, weight_space[row_tap, col_tap], pr...]
    ppermute x4 -> x0, starting transfers between devices: 19.8 us -> none  [the longest x2 13.3 us: extended(): after = lax.ppermute(initial, axis, down)]
    another operation x24 -> x0, local copies, waits for them, and re-layouts: 9.59 us -> none
    reshape x5 -> x0, local copies, waits for them, and re-layouts: 3.94 us -> none  [the longest x1 3.37 us: per_device(): sum_space.reshape(-1)]
  transfers between devices with their start and end apart: 5 -> 0, of which waited for: 4 -> 0; matrix products, arithmetic and copies ran while one was open for 2% -> 0% of each run, Pallas kernels for 0% -> 0%
where the time goes in v3:
time: 66.2 us; the launch traced here: 66.1 us
  Pallas kernels  65.4 us (99%)
    pallas_call x1, Pallas kernels, block(): pl.pallas_call(block_kernel, out_shape=[one] * 4 + [jax.ShapeDtypeStruct(...  63.4 us
    pallas_call x1, Pallas kernels, tail(): pl.pallas_call(lambda *refs: tail_kernel(factor, *refs), out_shape=[one]...  1.98 us

profile of v3, /device:TPU:1, one launch (start us, length us, event | category | flops | bytes accessed | tf_op | source)
XLA Modules:
  0.0 66.1 jit_solution(795368361467484643)
XLA Ops:
  0.6 63.4 %block.1 = (bf16[2,64,320]{2,1,0:T(8,128)(2,1)}, bf16[2,64,320]{2,1,0:T(8,128)(2,1)}, bf16[2,64,320]{2,1,0:T(8,128)(2,1)}, bf16[2,64,320]{2,1,0:T(8,128)(2,1)}, f32[8,3,8,128]{3,2,1,0:T(8,128)}) custom-call(bf16[2,64,320]{2,1,0:T(8,128)(2,1)} %bitcast.18, bf16[2,64,320]{2,1,0:T(8,128)(2,1)} %bitcast.19, bf16[2,64,320]{2,1,0:T(8,128)(2,1)} %bitcast.20, ...), custom_call_target="tpu_custom_call" | custom-call | tf_op jit(solution)/shard_map/block/pallas_call | solution.py:382
  64.1 2.0 %tail.1 = (bf16[2,64,320]{2,1,0:T(8,128)(2,1)}, bf16[2,64,320]{2,1,0:T(8,128)(2,1)}, bf16[2,64,320]{2,1,0:T(8,128)(2,1)}, bf16[2,64,320]{2,1,0:T(8,128)(2,1)}, f32[1,900]{1,0:T(1,128)}, /*index=5*/f32[1,480]{1,0:T(1,128)}) custom-call(bf16[2,64,320]{2,1,0:T(8,128)(2,1)} %get-tuple-element.17.refs_0_, bf16[2,64,320]{2,1,0:T(8,128)(2,1)} %get-tuple-element.18.refs_1_, ...), custom_call_target="tpu_custom_call" | custom-call | tf_op jit(solution)/shard_map/tail/pallas_call | solution.py:450

commit v4 on v3

--- a/solution.py
+++ b/solution.py
@@ -62,7 +62,7 @@
 
 def block_kernel(
     y1h, y2h, c1h, c2h, wsh, wth, xf, xs, gf, gs, out,
-    y1, y2, c1, c2, ws, wt, tb, hb, sq, cs, wide, pa, pg, sa, rq, g, gt, rt, s0, r1, s1, r2, s2, r3, fin,
+    y1, y2, c1, c2, ws, wt, tb, hb, sq, cs, wide, pa, pg, rq, g, gt, rt, s0, r1, s1, r2, s2, r3, fin,
     in_sem, t_snd, t_rcv, n_snd, n_rcv, r_snd, r_rcv, f_snd, f_rcv, q_snd, q_rcv, x_snd, x_rcv, y_snd, y_rcv, z_snd, z_rcv, g_snd, g_rcv,
 ):
     z, yl, x, yh, c = place()
@@ -93,7 +93,7 @@
 
     @pl.when(jnp.logical_not(has_far))
     def _():
-        hb[far] = jnp.zeros((2, 128, 320), BF16)
+        hb[far] = jnp.zeros((2, 5, 64, 128), BF16)
 
     for n, ref in enumerate((y1, c2)):
         loads[n].wait()
@@ -105,21 +105,20 @@
     tb[1, 1] = sq[1].astype(BF16)
     pl.semaphore_wait(barrier, met)
 
-    ahead_t = send(tb.at[1], tb.at[0], t_snd.at[0], t_rcv.at[0], ((tm + 1) % 32, row))
-    behind_t = send(tb.at[1], tb.at[2], t_snd.at[1], t_rcv.at[1], ((tm + 31) % 32, row))
+    ahead_t = [send(tb.at[1, n], tb.at[0, n], t_snd.at[n, 0], t_rcv.at[n, 0], ((tm + 1) % 32, row)) for n in range(2)]
+    behind_t = [send(tb.at[1, n], tb.at[2, n], t_snd.at[n, 1], t_rcv.at[n, 1], ((tm + 31) % 32, row)) for n in range(2)]
     has_next, has_last = jnp.logical_not(last_t), jnp.logical_not(first_t)
-    pl.when(has_next)(ahead_t.start)
-    pl.when(has_last)(behind_t.start)
-
-    def time_taps(ks):
-        for q in range(5):
-            at = pl.ds(q * 128, 128)
-            ahead, back = None, None
-            for k in ks:
-                one = dot(tb[k, 0, :, at], wt[k, q], 1, 0)
-                two = dot(tb[2 - k, 1, :, at], wt[k, q], 1, 1)
-                ahead, back = (one, two) if ahead is None else (ahead + one, back + two)
-            yield at, ahead, back
+    for n in range(2):
+        pl.when(has_next)(ahead_t[n].start)
+        pl.when(has_last)(behind_t[n].start)
+
+    def time_taps(n, ks, q):
+        at = pl.ds(q * 128, 128)
+        both = None
+        for k in ks:
+            one = dot(tb[k, 0, :, at], wt[k, q], 1, 0) if n == 0 else dot(tb[2 - k, 1, :, at], wt[k, q], 1, 1)
+            both = one if both is None else both + one
+        return both
 
     def time_terms(ks):
         for k in ks:
@@ -128,18 +127,20 @@
                 gt[pl.ds((k * 5 + q) * 16, 16)] = dot(tb[1, 0, :, at], tb[2 - k, 1, :, at], 0, 0).reshape(16, 8, 128)
 
     loads[2].wait()
-    for at, ahead, back in time_taps((1,)):
-        cs[0, :, at] = ahead
-        cs[1, :, at] = back
+    for n in range(2):
+        for q in range(5):
+            cs[n, :, pl.ds(q * 128, 128)] = time_taps(n, (1,), q)
     time_terms((1,))
     loads[3].wait()
     loads[4].wait()
-    pl.when(has_last)(ahead_t.wait_recv)
-    pl.when(has_next)(behind_t.wait_recv)
-    for at, ahead, back in time_taps((0, 2)):
-        cs[0, :, at] = cs[0, :, at] + ahead
-        cs[1, :, at] = (cs[1, :, at] + back) * slope(sq[0, :, at])
+    far_row, near_row = [], []
     for n, (src, res) in enumerate(((y2, xs), (c1, gf))):
+        pl.when(has_last)(ahead_t[n].wait_recv)
+        pl.when(has_next)(behind_t[n].wait_recv)
+        for q in range(5):
+            at = pl.ds(q * 128, 128)
+            whole = cs[n, :, at] + time_taps(n, (0, 2), q)
+            cs[n, :, at] = whole if n == 0 else whole * slope(sq[0, :, at])
         low, high = cs[n, :, 0:320], cs[n, :, 320:640]
         for f in range(2):
             part = ((low + high if f == 0 else low - high) * HAAR).astype(BF16).astype(F32)
@@ -149,11 +150,13 @@
             if n == 0:
                 w = new.astype(F32)
                 held = (w * sigmoid(w)).astype(BF16)
-            hb[own, n, pl.ds(f * 64, 64)] = held
-    far_row = send(hb.at[own], hb.at[3 - far], r_snd.at[0], r_rcv.at[0], (tm, (row + 2 * c + 15) % 16))
-    pl.when(has_far)(far_row.start)
-    near_row = send(hb.at[own], hb.at[own], n_snd.at[0], n_rcv.at[0], partner)
-    near_row.start()
+            hb[own, n, 2 * f] = held[:, 0:128]
+            hb[own, n, 2 * f + 1] = held[:, 128:256]
+            hb[own, n, 4, :, pl.ds(64 * f, 64)] = held[:, 256:320]
+        far_row.append(send(hb.at[own, n], hb.at[3 - far, n], r_snd.at[n], r_rcv.at[n], (tm, (row + 2 * c + 15) % 16)))
+        pl.when(has_far)(far_row[n].start)
+        near_row.append(send(hb.at[own, n], hb.at[own, n], n_snd.at[n], n_rcv.at[n], partner))
+        near_row[n].start()
 
     time_terms((0, 2))
 
@@ -179,11 +182,17 @@
         for copy in time_half:
             copy.start()
 
-    def spread(slot):
-        for n, ref in enumerate((pa, pg)):
-            wide[n] = hb[slot, n].astype(F32)
-            for q in range(2):
-                ref[slot, q, :, 8:72] = wide[n, :, pl.ds(q * 160, 160)].reshape(2, 64, 160)
+    def widen(slot, n):
+        for f in range(2):
+            at = pl.ds(f * 64, 64)
+            wide[n, at, 0:128] = hb[slot, n, 2 * f].astype(F32)
+            wide[n, at, 128:256] = hb[slot, n, 2 * f + 1].astype(F32)
+            wide[n, at, 256:320] = hb[slot, n, 4, :, pl.ds(64 * f, 64)].astype(F32)
+
+    def spread(slot, n):
+        widen(slot, n)
+        for q in range(2):
+            (pa, pg)[n][slot, q, :, 8:72] = wide[n, :, pl.ds(q * 160, 160)].reshape(2, 64, 160)
 
     def right_side(slot):
         for q in range(2):
@@ -192,11 +201,11 @@
                     c == 0, wide[1, :, pl.ds(q * 160 + 32 * n, 32)], wide[1, :, pl.ds(q * 160 + 128, 32)]
                 ).astype(BF16)
 
-    spread(own)
-    near_row.wait_recv()
-    spread(other)
-    for slot in (1, 2):
-        wide[1] = hb[slot, 1].astype(F32)
+    for slot in (own, other):
+        for n in range(2):
+            if slot is other:
+                near_row[n].wait_recv()
+            spread(slot, n)
         right_side(slot)
 
     def left(slot, b, q):
@@ -212,9 +221,9 @@
 
     lane = lax.broadcasted_iota(jnp.int32, (3, 8, 128), 2)
 
-    def pack_space(lo, hi):
+    def pack_space(lo, count):
         def pack(n, carry):
-            zz, yp = n // 4, n % 4
+            zz, yp = lo + n // 4, n % 4
             chunk = (zz + 8 - SHIFT) % 8 * 4 + yp
             tiles = g[pl.ds((45 * chunk) // 4, 12)]
 
@@ -230,12 +239,15 @@
 
             return carry
 
-        lax.fori_loop(lo * 4, hi * 4, pack, 0)
+        lax.fori_loop(0, count * 4, pack, 0)
+
+    def group(xp, yp):
+        return (xp + 4 - yp) % 4
 
     def along_x(k, j, part):
         xp, yp = (x + k) % 4, (yl + j) % 4
-        at = pl.ds(0, EARLY) if part == 0 else pl.ds(EARLY, 8 - EARLY)
-        return send(s0.at[xp, yp, at], r1.at[k - 1, yp, at], x_snd.at[k - 1, j, part], x_rcv.at[k - 1, j, part], ident(z, yl, xp, yh, c))
+        at = pl.ds(0, EARLY) if isinstance(part, int) and part == 0 else pl.ds(EARLY + 3 * (part - 1), 3)
+        return send(s0.at[group(xp, yp), yp, at], r1.at[k - 1, yp, at], x_snd.at[k - 1, j, part], x_rcv.at[k - 1, j, part], ident(z, yl, xp, yh, c))
 
     space_terms((1,))
 
@@ -247,61 +259,78 @@
                 s0[xp, yp] = (s0[xp, yp].astype(F32) + rt[xp - 1, yp].astype(F32)).astype(BF16)
 
     pack_space(0, EARLY)
-    timed = [jnp.logical_and(c == 1, (x + k) % 4 != 0) for k in range(4)]
-    for k in (1, 2, 3):
-        for j in (1, 2, 3, 0):
-            along_x(k, j, 0).start()
-            pl.when(timed[k])(along_x(k, j, 1).start)
-
-    pl.when(has_far)(far_row.wait_recv)
+    order = [(k, j) for j in (1, 2, 3, 0) for k in (2, 1, 3)]
+    timed = {(k, j): jnp.logical_and(c == 1, group((x + k) % 4, (yl + j) % 4) != 0) for k, j in order}
+    for k, j in order:
+        along_x(k, j, 0).start()
+
+        @pl.when(timed[k, j])
+        def _():
+            along_x(k, j, 1).start()
+            along_x(k, j, 2).start()
+
+    def late_part(part):
+        pack_space(EARLY + 3 * (part - 1), 3)
+        for k, j in order:
+            pl.when(jnp.logical_not(timed[k, j]))(along_x(k, j, part).start)
+
+
+    pl.when(has_far)(far_row[0].wait_recv)
     pass_on = send(hb.at[far, 0], hb.at[far, 0], f_snd.at[0], f_rcv.at[0], partner)
     pass_on.start()
-    spread(far)
-    for q in range(2):
-        ahead, back = None, None
-        for a in range(3):
-            for b in range(3):
-                moved = left(c + a, b, q)
-                one = dot(moved, ws_at(ws, loads, a, b, q), 1, 0)
-                moved = pg[c + 2 - a, q, :, pl.ds(9 - b, 64)].reshape(128, 160).astype(BF16)
-                two = dot(moved, ws[a, b, q], 1, 1)
-                ahead, back = (one, two) if ahead is None else (ahead + one, back + two)
-        sa[0, :, pl.ds(q * 160, 160)] = ahead
-        sa[1, :, pl.ds(q * 160, 160)] = back
+    spread(far, 0)
+    space_terms((2 * c,))
+    late_part(2 - c)
     pass_on.wait_recv()
-    wide[0] = hb[3 - far, 0].astype(F32)
-    for q in range(2):
-        pa[3 - far, q, :, 8:72] = wide[0, :, pl.ds(q * 160, 160)].reshape(2, 64, 160)
-    space_terms((0, 2))
-    pack_space(EARLY, 8)
-    for k in (1, 2, 3):
-        for j in (1, 2, 3, 0):
-            pl.when(jnp.logical_not(timed[k]))(along_x(k, j, 1).start)
-    for f in range(2):
-        at = pl.ds(f * 64, 64)
-        xf[f] = (y1[f].astype(F32) - sa[0, at]).astype(BF16)
-        gs[f] = (c2[f].astype(F32) + sa[1, at] * slope(xs[f].astype(F32))).astype(BF16)
-
-    third = {}
-    for j in (1, 2, 3, 0):
+    spread(3 - far, 0)
+    space_terms((2 - 2 * c,))
+    late_part(1 + c)
+
+    def along_y(j, h):
+        yp, hp = (yl + j) % 4, (yh + h) % 2
+        return send(s1.at[yp, pl.ds(hp * 4, 4)], r2.at[2 * j + h], y_snd.at[2 * j + h], y_rcv.at[2 * j + h], ident(z, yp, x, hp, c))
+
+    def sum_x(j):
         yp = (yl + j) % 4
         for k in (1, 2, 3):
-            for part in range(2):
+            for part in range(3):
                 along_x(k, j, part).wait_recv()
-        total = s0[x, yp].astype(F32)
+        total = s0[group(x, yp), yp].astype(F32)
         for k in (1, 2, 3):
             total += r1[k - 1, yp].astype(F32)
         s1[yp] = total.astype(BF16)
         for h in (1, 0):
             if j or h:
-                hp = (yh + h) % 2
-                copy = send(s1.at[yp, pl.ds(hp * 4, 4)], r2.at[2 * j + h], y_snd.at[2 * j + h], y_rcv.at[2 * j + h], ident(z, yp, x, hp, c))
-                copy.start()
-                third[j, h] = copy
+                along_y(j, h).start()
+
+    for early in (True, False):
+        for j in (1, 2, 3, 0):
+            is_time = jnp.logical_and(c == 1, group(x, (yl + j) % 4) != 0)
+            pl.when(is_time if early else jnp.logical_not(is_time))(lambda j=j: sum_x(j))
+
+    pl.when(has_far)(far_row[1].wait_recv)
+    spread(far, 1)
+    loads[5].wait()
+    for q in range(2):
+        ahead, back = None, None
+        for a in range(3):
+            for b in range(3):
+                one = dot(left(c + a, b, q), ws[a, b, q], 1, 0)
+                moved = pg[c + 2 - a, q, :, pl.ds(9 - b, 64)].reshape(128, 160).astype(BF16)
+                two = dot(moved, ws[a, b, q], 1, 1)
+                ahead, back = (one, two) if ahead is None else (ahead + one, back + two)
+        wide[0, :, pl.ds(q * 160, 160)] = ahead
+        wide[1, :, pl.ds(q * 160, 160)] = back
+    for f in range(2):
+        at = pl.ds(f * 64, 64)
+        xf[f] = (y1[f].astype(F32) - wide[0, at]).astype(BF16)
+        gs[f] = (c2[f].astype(F32) + wide[1, at] * slope(xs[f].astype(F32))).astype(BF16)
+
     total = s1[yl, pl.ds(yh * 4, 4)].astype(F32)
-    for j, h in third:
-        third[j, h].wait_recv()
-    for j, h in third:
+    others = [(j, h) for j in (1, 2, 3, 0) for h in (1, 0) if j or h]
+    for j, h in others:
+        along_y(j, h).wait_recv()
+    for j, h in others:
         total += r2[2 * j + h].astype(F32)
     s2[...] = total.astype(BF16)
 
@@ -313,14 +342,21 @@
         copy = send(s2.at[zz % 4], r3.at[d - 1], z_snd.at[d - 1], z_rcv.at[d - 1], ident(zp, yl, x, yh, c))
         pl.when(zz // 4 == yh)(copy.wait_send if finish else copy.start)
 
+    def takes(slot, to):
+        space, time = 90 * tm % 8 + 900 * to // 160, 60 * tm % 8 + 480 * to // 128
+        low = 24 * (slot % 5)
+        main = jnp.logical_and(space <= low + 23, space + 6 >= low)
+        late = jnp.logical_and(time <= low + 23, time + 4 >= low)
+        return jnp.logical_or(slot == 4, jnp.logical_or(jnp.logical_and(slot < 4, main), jnp.logical_and(slot > 4, late)))
+
+    offsets = [(dx, h, dc) for dx in (2, 1, 3, 0) for h in (1, 0) for dc in (1, 0) if dx or h or dc]
+
     def over_row(finish):
-        for dx in range(4):
-            for h in range(2):
-                for dc in range(2):
-                    if dx or h or dc:
-                        n = dx * 2 + dc
-                        copy = send(fin.at[c * 4 + x], fin.at[c * 4 + x], g_snd.at[n, h], g_rcv.at[n], ident(z, yl, (x + dx) % 4, (yh + h) % 2, (c + dc) % 2))
-                        copy.wait_send() if finish else copy.start()
+        slot = c * 4 + group(x, yl)
+        for dx, h, dc in offsets:
+            n, xp, hp, cp = dx * 2 + dc, (x + dx) % 4, (yh + h) % 2, (c + dc) % 2
+            copy = send(fin.at[slot], fin.at[slot], g_snd.at[n, h], g_rcv.at[n], ident(z, yl, xp, hp, cp))
+            pl.when(takes(slot, xp * 4 + hp * 2 + cp))(copy.wait_send if finish else copy.start)
 
     for d in range(1, 8):
         along_z(d, False)
@@ -332,13 +368,14 @@
         last = s2[(z + SHIFT) % 4].astype(F32)
         for d in range(1, 8):
             last += r3[d - 1].astype(F32)
-        fin[c * 4 + x] = last
+        fin[c * 4 + group(x, yl)] = last
         over_row(False)
 
-    pl.when(has_next)(ahead_t.wait_send)
-    pl.when(has_last)(behind_t.wait_send)
-    pl.when(has_far)(far_row.wait_send)
-    near_row.wait_send()
+    for n in range(2):
+        pl.when(has_next)(ahead_t[n].wait_send)
+        pl.when(has_last)(behind_t[n].wait_send)
+        pl.when(has_far)(far_row[n].wait_send)
+        near_row[n].wait_send()
     pass_on.wait_send()
 
     @pl.when(c == 0)
@@ -348,30 +385,22 @@
 
     for k in (1, 2, 3):
         for j in range(4):
-            for part in range(2):
+            for part in range(3):
                 along_x(k, j, part).wait_send()
-    for copy in third.values():
-        copy.wait_send()
+    for j, h in others:
+        along_y(j, h).wait_send()
     for d in range(1, 8):
         along_z(d, True)
 
     for dx in range(4):
         for dc in range(2):
             n = dx * 2 + dc
-            src = (c + dc) % 2 * 4 + (x - dx) % 4
+            src = (c + dc) % 2 * 4 + group((x + 4 - dx) % 4, yl)
             copy = send(fin.at[src], fin.at[src], g_snd.at[n, 1], g_rcv.at[n], ident(z, yl, (x + dx) % 4, 1 - yh, (c + dc) % 2))
-            if n:
-                copy.wait_recv()
-            else:
-                pl.when(jnp.logical_not(mine))(copy.wait_recv)
+            wanted = takes(src, row)
+            pl.when(wanted if n else jnp.logical_and(wanted, jnp.logical_not(mine)))(copy.wait_recv)
     out[...] = fin[...]
     pl.when(mine)(lambda: over_row(True))
-
-
-def ws_at(ws, loads, a, b, q):
-    if (a, b, q) == (0, 0, 0):
-        loads[5].wait()
-    return ws[a, b, q]
 
 
 def block(y1, y2, c1, c2, ws, wt):
@@ -389,13 +418,12 @@
             vm((3, 3, 2, 160, 160), BF16),
             vm((3, 5, 128, 128), BF16),
             vm((3, 2, 64, 640), BF16),
-            vm((4, 2, 128, 320), BF16),
+            vm((4, 2, 5, 64, 128), BF16),
             vm((2, 64, 640), F32),
             vm((2, 64, 640), F32),
             vm((2, 128, 320), F32),
             vm((4, 2, 2, 80, 160), F32),
             vm((4, 2, 2, 80, 160), F32),
-            vm((2, 128, 320), F32),
             vm((2, 2, 128, 128), BF16),
             vm((360, 8, 128), F32),
             vm((240, 8, 128), F32),
@@ -409,10 +437,11 @@
             vm((8, 3, 8, 128), F32),
         ]
         + [dma((6,))]
-        + [dma((2,))] * 2
-        + [dma((1,))] * 6
+        + [dma((2, 2))] * 2
+        + [dma((2,))] * 4
+        + [dma((1,))] * 2
         + [dma((3,))] * 2
-        + [dma((3, 4, 2))] * 2
+        + [dma((3, 4, 3))] * 2
         + [dma((8,))] * 2
         + [dma((7,))] * 2
         + [dma((8, 2)), dma((8,))],

time: 66.2 us -> 60.8 us (0.918)
  Pallas kernels: 65.4 us -> 59.5 us
    pallas_call x1, Pallas kernels: 63.4 us -> 57.6 us  [block(): pl.pallas_call(block_kernel, out_shape=[one] * 4 + [jax.ShapeDtypeStruct(...]
where the time goes in v4:
time: 60.8 us; the launch traced here: 60.2 us
  Pallas kernels  59.5 us (98%)
  between operations  0.64 us (1%)
    pallas_call x1, Pallas kernels, block(): pl.pallas_call(block_kernel, out_shape=[one] * 4 + [jax.ShapeDtypeStruct(...  57.6 us
    pallas_call x1, Pallas kernels, tail(): pl.pallas_call(lambda *refs: tail_kernel(factor, *refs), out_shape=[one]...  1.98 us

profile of v4, /device:TPU:1, one launch (start us, length us, event | category | flops | bytes accessed | tf_op | source)
XLA Modules:
  0.0 60.2 jit_solution(10210760660541438615)
XLA Ops:
  0.6 57.6 %block.1 = (bf16[2,64,320]{2,1,0:T(8,128)(2,1)}, bf16[2,64,320]{2,1,0:T(8,128)(2,1)}, bf16[2,64,320]{2,1,0:T(8,128)(2,1)}, bf16[2,64,320]{2,1,0:T(8,128)(2,1)}, f32[8,3,8,128]{3,2,1,0:T(8,128)}) custom-call(bf16[2,64,320]{2,1,0:T(8,128)(2,1)} %bitcast.18, bf16[2,64,320]{2,1,0:T(8,128)(2,1)} %bitcast.19, bf16[2,64,320]{2,1,0:T(8,128)(2,1)} %bitcast.20, ...), custom_call_target="tpu_custom_call" | custom-call | tf_op jit(solution)/shard_map/block/pallas_call | solution.py:411
  58.2 2.0 %tail.1 = (bf16[2,64,320]{2,1,0:T(8,128)(2,1)}, bf16[2,64,320]{2,1,0:T(8,128)(2,1)}, bf16[2,64,320]{2,1,0:T(8,128)(2,1)}, bf16[2,64,320]{2,1,0:T(8,128)(2,1)}, f32[1,900]{1,0:T(1,128)}, /*index=5*/f32[1,480]{1,0:T(1,128)}) custom-call(bf16[2,64,320]{2,1,0:T(8,128)(2,1)} %get-tuple-element.17.refs_0_, bf16[2,64,320]{2,1,0:T(8,128)(2,1)} %get-tuple-element.18.refs_1_, ...), custom_call_target="tpu_custom_call" | custom-call | tf_op jit(solution)/shard_map/tail/pallas_call | solution.py:479

commit v5 on v4

--- a/solution.py
+++ b/solution.py
@@ -47,7 +47,7 @@
     for dx in range(4):
         for h in range(2):
             for dc in range(2):
-                if dx or h or dc:
+                if (dx > 0) + h + dc == 1:
                     peers.append(ident(z, yl, (x + dx) % 4, (yh + h) % 2, (c + dc) % 2))
     for j in range(1, 4):
         for h in range(2):
@@ -61,9 +61,9 @@
 
 
 def block_kernel(
-    y1h, y2h, c1h, c2h, wsh, wth, xf, xs, gf, gs, out,
-    y1, y2, c1, c2, ws, wt, tb, hb, sq, cs, wide, pa, pg, rq, g, gt, rt, s0, r1, s1, r2, s2, r3, fin,
-    in_sem, t_snd, t_rcv, n_snd, n_rcv, r_snd, r_rcv, f_snd, f_rcv, q_snd, q_rcv, x_snd, x_rcv, y_snd, y_rcv, z_snd, z_rcv, g_snd, g_rcv,
+    y1h, y2h, c1h, c2h, wsh, wth, xfh, xsh, gfh, gsh, out,
+    xf, xs, gf, gs,    y1, y2, c1, c2, ws, wt, tb, hb, sq, cs, wide, pa, pg, rq, g, gt, rt, s0, r1, s1, r2, s2, r3, fin,
+    in_sem, out_sem, t_snd, t_rcv, n_snd, n_rcv, r_snd, r_rcv, f_snd, f_rcv, q_snd, q_rcv, x_snd, x_rcv, y_snd, y_rcv, z_snd, z_rcv, g_snd, g_rcv,
 ):
     z, yl, x, yh, c = place()
     tm, row = z * 4 + yl, x * 4 + yh * 2 + c
@@ -73,16 +73,12 @@
     ]
     for load in loads:
         load.start()
+    stores = [pltpu.make_async_copy(src, dst, out_sem.at[n]) for n, (src, dst) in enumerate(((xf, xfh), (xs, xsh), (gf, gfh), (gs, gsh)))]
     barrier, met = greet(z, yl, x, yh, c)
     partner = ident(z, yl, x, yh, 1 - c)
     first_t, last_t = tm == 0, tm == 31
     own, other, far = 1 + c, 2 - c, 3 * c
     has_far = jnp.logical_not(jnp.logical_or(row == 0, row == 15))
-    pad = jnp.zeros((4, 2, 2, 8, 160), F32)
-    for ref in (pa, pg):
-        ref[:, :, :, 0:8] = pad
-        ref[:, :, :, 72:80] = pad
-
     @pl.when(first_t)
     def _():
         tb[0] = jnp.zeros((2, 64, 640), BF16)
@@ -94,23 +90,27 @@
     @pl.when(jnp.logical_not(has_far))
     def _():
         hb[far] = jnp.zeros((2, 5, 64, 128), BF16)
+
+    ahead_t = [send(tb.at[1, n], tb.at[0, n], t_snd.at[n, 0], t_rcv.at[n, 0], ((tm + 1) % 32, row)) for n in range(2)]
+    behind_t = [send(tb.at[1, n], tb.at[2, n], t_snd.at[n, 1], t_rcv.at[n, 1], ((tm + 31) % 32, row)) for n in range(2)]
+    has_next, has_last = jnp.logical_not(last_t), jnp.logical_not(first_t)
 
     for n, ref in enumerate((y1, c2)):
         loads[n].wait()
         even, odd = ref[0].astype(F32), ref[1].astype(F32)
         sq[n, :, 0:320] = (even + odd) * HAAR
         sq[n, :, 320:640] = (even - odd) * HAAR
-    v = sq[0]
-    tb[1, 0] = (v * sigmoid(v)).astype(BF16)
-    tb[1, 1] = sq[1].astype(BF16)
-    pl.semaphore_wait(barrier, met)
-
-    ahead_t = [send(tb.at[1, n], tb.at[0, n], t_snd.at[n, 0], t_rcv.at[n, 0], ((tm + 1) % 32, row)) for n in range(2)]
-    behind_t = [send(tb.at[1, n], tb.at[2, n], t_snd.at[n, 1], t_rcv.at[n, 1], ((tm + 31) % 32, row)) for n in range(2)]
-    has_next, has_last = jnp.logical_not(last_t), jnp.logical_not(first_t)
-    for n in range(2):
+        v = sq[n]
+        tb[1, n] = (v * sigmoid(v) if n == 0 else v).astype(BF16)
+        if n == 0:
+            pl.semaphore_wait(barrier, met)
         pl.when(has_next)(ahead_t[n].start)
         pl.when(has_last)(behind_t[n].start)
+
+    pad = jnp.zeros((4, 2, 2, 8, 160), F32)
+    for ref in (pa, pg):
+        ref[:, :, :, 0:8] = pad
+        ref[:, :, :, 72:80] = pad
 
     def time_taps(n, ks, q):
         at = pl.ds(q * 128, 128)
@@ -157,6 +157,7 @@
         pl.when(has_far)(far_row[n].start)
         near_row.append(send(hb.at[own, n], hb.at[own, n], n_snd.at[n], n_rcv.at[n], partner))
         near_row[n].start()
+        stores[1 + n].start()
 
     time_terms((0, 2))
 
@@ -307,6 +308,41 @@
         for j in (1, 2, 3, 0):
             is_time = jnp.logical_and(c == 1, group(x, (yl + j) % 4) != 0)
             pl.when(is_time if early else jnp.logical_not(is_time))(lambda j=j: sum_x(j))
+
+    total = s1[yl, pl.ds(yh * 4, 4)].astype(F32)
+    others = [(j, h) for j in (1, 2, 3, 0) for h in (1, 0) if j or h]
+    for j, h in others:
+        along_y(j, h).wait_recv()
+    for j, h in others:
+        total += r2[2 * j + h].astype(F32)
+    s2[...] = total.astype(BF16)
+
+    mine = (z + SHIFT) % 8 // 4 == yh
+
+    def along_z(d, finish):
+        zp = (z + d) % 8
+        zz = (zp + SHIFT) % 8
+        copy = send(s2.at[zz % 4], r3.at[d - 1], z_snd.at[d - 1], z_rcv.at[d - 1], ident(zp, yl, x, yh, c))
+        pl.when(zz // 4 == yh)(copy.wait_send if finish else copy.start)
+
+    def takes(slot, to):
+        space, time = 90 * tm % 8 + 900 * to // 160, 60 * tm % 8 + 480 * to // 128
+        low = 24 * (slot % 5)
+        main = jnp.logical_and(space <= low + 23, space + 6 >= low)
+        late = jnp.logical_and(time <= low + 23, time + 4 >= low)
+        return jnp.logical_or(slot == 4, jnp.logical_or(jnp.logical_and(slot < 4, main), jnp.logical_and(slot > 4, late)))
+
+    offsets = [(dx, h, dc) for dx in (2, 1, 3, 0) for h in (1, 0) for dc in (1, 0) if dx or h or dc]
+
+    def over_row(finish):
+        slot = c * 4 + group(x, yl)
+        for dx, h, dc in offsets:
+            n, xp, hp, cp = dx * 2 + dc, (x + dx) % 4, (yh + h) % 2, (c + dc) % 2
+            copy = send(fin.at[slot], fin.at[slot], g_snd.at[n, h], g_rcv.at[n], ident(z, yl, xp, hp, cp))
+            pl.when(takes(slot, xp * 4 + hp * 2 + cp))(copy.wait_send if finish else copy.start)
+
+    for d in range(1, 8):
+        along_z(d, False)
 
     pl.when(has_far)(far_row[1].wait_recv)
     spread(far, 1)
@@ -325,41 +361,8 @@
         at = pl.ds(f * 64, 64)
         xf[f] = (y1[f].astype(F32) - wide[0, at]).astype(BF16)
         gs[f] = (c2[f].astype(F32) + wide[1, at] * slope(xs[f].astype(F32))).astype(BF16)
-
-    total = s1[yl, pl.ds(yh * 4, 4)].astype(F32)
-    others = [(j, h) for j in (1, 2, 3, 0) for h in (1, 0) if j or h]
-    for j, h in others:
-        along_y(j, h).wait_recv()
-    for j, h in others:
-        total += r2[2 * j + h].astype(F32)
-    s2[...] = total.astype(BF16)
-
-    mine = (z + SHIFT) % 8 // 4 == yh
-
-    def along_z(d, finish):
-        zp = (z + d) % 8
-        zz = (zp + SHIFT) % 8
-        copy = send(s2.at[zz % 4], r3.at[d - 1], z_snd.at[d - 1], z_rcv.at[d - 1], ident(zp, yl, x, yh, c))
-        pl.when(zz // 4 == yh)(copy.wait_send if finish else copy.start)
-
-    def takes(slot, to):
-        space, time = 90 * tm % 8 + 900 * to // 160, 60 * tm % 8 + 480 * to // 128
-        low = 24 * (slot % 5)
-        main = jnp.logical_and(space <= low + 23, space + 6 >= low)
-        late = jnp.logical_and(time <= low + 23, time + 4 >= low)
-        return jnp.logical_or(slot == 4, jnp.logical_or(jnp.logical_and(slot < 4, main), jnp.logical_and(slot > 4, late)))
-
-    offsets = [(dx, h, dc) for dx in (2, 1, 3, 0) for h in (1, 0) for dc in (1, 0) if dx or h or dc]
-
-    def over_row(finish):
-        slot = c * 4 + group(x, yl)
-        for dx, h, dc in offsets:
-            n, xp, hp, cp = dx * 2 + dc, (x + dx) % 4, (yh + h) % 2, (c + dc) % 2
-            copy = send(fin.at[slot], fin.at[slot], g_snd.at[n, h], g_rcv.at[n], ident(z, yl, xp, hp, cp))
-            pl.when(takes(slot, xp * 4 + hp * 2 + cp))(copy.wait_send if finish else copy.start)
-
-    for d in range(1, 8):
-        along_z(d, False)
+    stores[0].start()
+    stores[3].start()
 
     @pl.when(mine)
     def _():
@@ -371,6 +374,8 @@
         fin[c * 4 + group(x, yl)] = last
         over_row(False)
 
+    for store in stores:
+        store.wait()
     for n in range(2):
         pl.when(has_next)(ahead_t[n].wait_send)
         pl.when(has_last)(behind_t[n].wait_send)
@@ -412,8 +417,8 @@
         block_kernel,
         out_shape=[one] * 4 + [jax.ShapeDtypeStruct((8, 3, 8, 128), F32)],
         in_specs=[there] * 6,
-        out_specs=[here] * 5,
-        scratch_shapes=[vm((2, 64, 320), BF16)] * 4
+        out_specs=[there] * 4 + [here],
+        scratch_shapes=[vm((2, 64, 320), BF16)] * 8
         + [
             vm((3, 3, 2, 160, 160), BF16),
             vm((3, 5, 128, 128), BF16),
@@ -436,7 +441,7 @@
             vm((7, 3, 8, 128), BF16),
             vm((8, 3, 8, 128), F32),
         ]
-        + [dma((6,))]
+        + [dma((6,)), dma((4,))]
         + [dma((2, 2))] * 2
         + [dma((2,))] * 4
         + [dma((1,))] * 2

time: 60.8 us -> 60.3 us (level)
  Pallas kernels: 59.5 us -> 58.7 us
    pallas_call x1, Pallas kernels: 57.6 us -> 56.7 us  [block(): pl.pallas_call(block_kernel, out_shape=[one] * 4 + [jax.ShapeDtypeStruct(...]
where the time goes in v5:
time: 60.3 us; the launch traced here: 59.3 us
  Pallas kernels  58.7 us (97%)
  between operations  0.64 us (1%)
    pallas_call x1, Pallas kernels, block(): pl.pallas_call(block_kernel, out_shape=[one] * 4 + [jax.ShapeDtypeStruct(...  56.7 us
    pallas_call x1, Pallas kernels, tail(): pl.pallas_call(lambda *refs: tail_kernel(factor, *refs), out_shape=[one]...  1.98 us

profile of v5, /device:TPU:1, one launch (start us, length us, event | category | flops | bytes accessed | tf_op | source)
XLA Modules:
  0.0 59.3 jit_solution(9399421964035060699)
XLA Ops:
  0.6 56.7 %block.1 = (bf16[2,64,320]{2,1,0:T(8,128)(2,1)}, bf16[2,64,320]{2,1,0:T(8,128)(2,1)}, bf16[2,64,320]{2,1,0:T(8,128)(2,1)}, bf16[2,64,320]{2,1,0:T(8,128)(2,1)}, f32[8,3,8,128]{3,2,1,0:T(8,128)}) custom-call(bf16[2,64,320]{2,1,0:T(8,128)(2,1)} %bitcast.18, bf16[2,64,320]{2,1,0:T(8,128)(2,1)} %bitcast.19, bf16[2,64,320]{2,1,0:T(8,128)(2,1)} %bitcast.20, ...), custom_call_target="tpu_custom_call" | custom-call | tf_op jit(solution)/shard_map/block/pallas_call | solution.py:416
  57.3 2.0 %tail.1 = (bf16[2,64,320]{2,1,0:T(8,128)(2,1)}, bf16[2,64,320]{2,1,0:T(8,128)(2,1)}, bf16[2,64,320]{2,1,0:T(8,128)(2,1)}, bf16[2,64,320]{2,1,0:T(8,128)(2,1)}, f32[1,900]{1,0:T(1,128)}, /*index=5*/f32[1,480]{1,0:T(1,128)}) custom-call(bf16[2,64,320]{2,1,0:T(8,128)(2,1)} %get-tuple-element.17.refs_0_, bf16[2,64,320]{2,1,0:T(8,128)(2,1)} %get-tuple-element.18.refs_1_, ...), custom_call_target="tpu_custom_call" | custom-call | tf_op jit(solution)/shard_map/tail/pallas_call | solution.py:484

commit v6 on v5

--- a/solution.py
+++ b/solution.py
@@ -325,12 +325,19 @@
         copy = send(s2.at[zz % 4], r3.at[d - 1], z_snd.at[d - 1], z_rcv.at[d - 1], ident(zp, yl, x, yh, c))
         pl.when(zz // 4 == yh)(copy.wait_send if finish else copy.start)
 
-    def takes(slot, to):
+    def takes(slot, to, t):
         space, time = 90 * tm % 8 + 900 * to // 160, 60 * tm % 8 + 480 * to // 128
-        low = 24 * (slot % 5)
-        main = jnp.logical_and(space <= low + 23, space + 6 >= low)
-        late = jnp.logical_and(time <= low + 23, time + 4 >= low)
-        return jnp.logical_or(slot == 4, jnp.logical_or(jnp.logical_and(slot < 4, main), jnp.logical_and(slot > 4, late)))
+
+        def meets(start, count, low):
+            return jnp.logical_and(start <= low + 7, start + count - 1 >= low)
+
+        low = 24 * (slot % 5) + 8 * t
+        rest = meets(space, 7, 8 * t)
+        for n in range(1, 4):
+            rest = jnp.logical_or(rest, meets(space, 7, 24 * n + 8 * t))
+        main = jnp.logical_and(slot < 4, meets(space, 7, low))
+        late = jnp.logical_and(slot > 4, meets(time, 5, low))
+        return jnp.logical_or(jnp.logical_and(slot == 4, rest), jnp.logical_or(main, late))
 
     offsets = [(dx, h, dc) for dx in (2, 1, 3, 0) for h in (1, 0) for dc in (1, 0) if dx or h or dc]
 
@@ -338,8 +345,9 @@
         slot = c * 4 + group(x, yl)
         for dx, h, dc in offsets:
             n, xp, hp, cp = dx * 2 + dc, (x + dx) % 4, (yh + h) % 2, (c + dc) % 2
-            copy = send(fin.at[slot], fin.at[slot], g_snd.at[n, h], g_rcv.at[n], ident(z, yl, xp, hp, cp))
-            pl.when(takes(slot, xp * 4 + hp * 2 + cp))(copy.wait_send if finish else copy.start)
+            for t in range(3):
+                copy = send(fin.at[slot, t], fin.at[slot, t], g_snd.at[n, h, t], g_rcv.at[n, t], ident(z, yl, xp, hp, cp))
+                pl.when(takes(slot, xp * 4 + hp * 2 + cp, t))(copy.wait_send if finish else copy.start)
 
     for d in range(1, 8):
         along_z(d, False)
@@ -401,9 +409,10 @@
         for dc in range(2):
             n = dx * 2 + dc
             src = (c + dc) % 2 * 4 + group((x + 4 - dx) % 4, yl)
-            copy = send(fin.at[src], fin.at[src], g_snd.at[n, 1], g_rcv.at[n], ident(z, yl, (x + dx) % 4, 1 - yh, (c + dc) % 2))
-            wanted = takes(src, row)
-            pl.when(wanted if n else jnp.logical_and(wanted, jnp.logical_not(mine)))(copy.wait_recv)
+            for t in range(3):
+                copy = send(fin.at[src, t], fin.at[src, t], g_snd.at[n, 1, t], g_rcv.at[n, t], ident(z, yl, (x + dx) % 4, 1 - yh, (c + dc) % 2))
+                wanted = takes(src, row, t)
+                pl.when(wanted if n else jnp.logical_and(wanted, jnp.logical_not(mine)))(copy.wait_recv)
     out[...] = fin[...]
     pl.when(mine)(lambda: over_row(True))
 
@@ -449,7 +458,7 @@
         + [dma((3, 4, 3))] * 2
         + [dma((8,))] * 2
         + [dma((7,))] * 2
-        + [dma((8, 2)), dma((8,))],
+        + [dma((8, 2, 3)), dma((8, 3))],
         compiler_params=pltpu.CompilerParams(collective_id=5, has_side_effects=True, vmem_limit_bytes=60 * 1024 * 1024),
         name="block",
     )(y1, y2, c1, c2, ws, wt)

time: 60.3 us -> 60.6 us (level)
  Pallas kernels: 58.7 us -> 59.5 us
    pallas_call x1, Pallas kernels: 56.7 us -> 57.5 us  [block(): pl.pallas_call(block_kernel, out_shape=[one] * 4 + [jax.ShapeDtypeStruct(...]
where the time goes in v6:
time: 60.6 us; the launch traced here: 60.2 us
  Pallas kernels  59.5 us (98%)
  between operations  0.64 us (1%)
    pallas_call x1, Pallas kernels, block(): pl.pallas_call(block_kernel, out_shape=[one] * 4 + [jax.ShapeDtypeStruct(...  57.5 us
    pallas_call x1, Pallas kernels, tail(): pl.pallas_call(lambda *refs: tail_kernel(factor, *refs), out_shape=[one]...  1.98 us

profile of v6, /device:TPU:1, one launch (start us, length us, event | category | flops | bytes accessed | tf_op | source)
XLA Modules:
  0.0 60.2 jit_solution(14332196158726724477)
XLA Ops:
  0.6 57.5 %block.1 = (bf16[2,64,320]{2,1,0:T(8,128)(2,1)}, bf16[2,64,320]{2,1,0:T(8,128)(2,1)}, bf16[2,64,320]{2,1,0:T(8,128)(2,1)}, bf16[2,64,320]{2,1,0:T(8,128)(2,1)}, f32[8,3,8,128]{3,2,1,0:T(8,128)}) custom-call(bf16[2,64,320]{2,1,0:T(8,128)(2,1)} %bitcast.18, bf16[2,64,320]{2,1,0:T(8,128)(2,1)} %bitcast.19, bf16[2,64,320]{2,1,0:T(8,128)(2,1)} %bitcast.20, ...), custom_call_target="tpu_custom_call" | custom-call | tf_op jit(solution)/shard_map/block/pallas_call | solution.py:425
  58.2 2.0 %tail.1 = (bf16[2,64,320]{2,1,0:T(8,128)(2,1)}, bf16[2,64,320]{2,1,0:T(8,128)(2,1)}, bf16[2,64,320]{2,1,0:T(8,128)(2,1)}, bf16[2,64,320]{2,1,0:T(8,128)(2,1)}, f32[1,900]{1,0:T(1,128)}, /*index=5*/f32[1,480]{1,0:T(1,128)}) custom-call(bf16[2,64,320]{2,1,0:T(8,128)(2,1)} %get-tuple-element.17.refs_0_, bf16[2,64,320]{2,1,0:T(8,128)(2,1)} %get-tuple-element.18.refs_1_, ...), custom_call_target="tpu_custom_call" | custom-call | tf_op jit(solution)/shard_map/tail/pallas_call | solution.py:493
